TPU v7x, 512 devices: a whole 4x4x16 slice. The times are simulated.
512 devices in a mesh: section: 8 (over y, core), mp: 64 (over z, x).
Axes of the slice: x: 4, y: 4, z: 16, core: 2. Of those that a mesh axis runs over, the one named last changes fastest.
Arguments:
- features: bfloat16 [4, 32, 8192], P(None, None, 'mp'), may hold values from -6 to 6
- labels: int32 [4, 32], replicated, may hold values 0 or 1
- weights: bfloat16 [8, 8192, 8192], P('section', None, 'mp'), may hold values from -1.78986404 to 1.78986404
- vectors: float32 [8, 8192], P('section', 'mp'), may hold values from -6 to 6
- head_weight: float32 [8192], P('mp'), may hold values from -0.0625 to 0.0625
Outputs:
- weight_grad: bfloat16 [8, 8192, 8192], P('section', None, 'mp')
- new_vectors: float32 [8, 8192], P('section', 'mp')
- rank_coef: float32 [8], P('section')
All inputs are finite; a program needn't handle non-finite values.
Results may differ from a plain program's by a relative error of at most 0.015.
Values may be sent and summed in bfloat16 or wider, within the bound.
A program may use at most 64 MiB of HBM per device.

v0:
```python
import functools

import jax
import jax.numpy as jnp
from jax import lax
from jax.sharding import Mesh
from jax.sharding import PartitionSpec as P

MP = ("mp_0", "mp_1")


loss_scale = 32.0
tiny_eps = 1e-06


def by_axis(shard, axes):
    return functools.reduce(lax.psum, axes, shard)


def from_everyone(shard, axis):
    devices = lax.axis_size(axis)
    return lax.all_to_all(
        jnp.broadcast_to(shard[None], (devices, *shard.shape)), axis, 0, 0, tiled=True
    )


def in_order(tiles, dim):
    tiles = jnp.moveaxis(tiles, 0, dim)
    lengths = tiles.shape
    return tiles.reshape(*lengths[:dim], lengths[dim] * lengths[dim + 1], *lengths[dim + 2 :])


def gather_directly(shard, axis, dim):
    tiles = from_everyone(shard, axis)
    return in_order(tiles, dim)


def shifted(block, axis, distance):
    devices = range(lax.axis_size(axis))
    route = [(i - distance, i) for i in devices if i - distance in devices]
    return lax.ppermute(block, axis, route)


def silu_slope(pre_act):
    gate_val = jax.nn.sigmoid(pre_act)
    return gate_val * (1.0 + pre_act * (1.0 - gate_val))


def keep_slot(stored, update, micro_slot, is_live):
    previous = lax.dynamic_index_in_dim(stored, micro_slot, 0, keepdims=False)
    return lax.dynamic_update_index_in_dim(
        stored, jnp.where(is_live, update, previous), micro_slot, 0
    )


def power_step(weight, vector_u):
    vector_bf = vector_u.astype(jnp.bfloat16)
    left_sum = by_axis(jnp.dot(weight, vector_bf, preferred_element_type=jnp.float32), MP)
    vector_v = (left_sum * lax.rsqrt(jnp.sum(left_sum * left_sum) + tiny_eps)).astype(jnp.bfloat16)
    right_part = jnp.dot(vector_v, weight, preferred_element_type=jnp.float32)
    norm_total = by_axis(jnp.sum(right_part * right_part), MP)
    spectral = jnp.sqrt(norm_total + tiny_eps)
    return (spectral, right_part / spectral)


def on_device(features, labels, weights, vectors, head_weight):
    weight = weights[0]
    vector_u = vectors[0]
    micro_count, batch_rows, local_cols = features.shape
    full_width = weight.shape[0]
    sections = lax.axis_size("section")
    section_index = lax.axis_index("section")
    tick_count = micro_count + sections - 1
    sign_all = (2 * labels - 1).astype(jnp.float32)
    spectral_init, new_init = power_step(weight, vector_u)

    def forward_tick(tick_now, state_all):
        incoming, inputs_all, pre_all, logits_all, spectral, new_u = state_all
        micro_index = tick_now - section_index
        is_live = (micro_index >= 0) & (micro_index < micro_count)
        micro_slot = jnp.clip(micro_index, 0, micro_count - 1)
        first_input = lax.dynamic_index_in_dim(features, micro_slot, 0, keepdims=False)
        layer_in = jnp.where(section_index == 0, first_input, incoming)
        shard_piece = gather_directly(layer_in, MP, 1)
        accum_part = jnp.dot(shard_piece, weight, preferred_element_type=jnp.float32)
        whole_rows = shard_piece
        accum_part, whole_rows = (accum_part, whole_rows)
        pre_act = accum_part / spectral
        layer_out = (layer_in.astype(jnp.float32) + jax.nn.silu(pre_act)).astype(jnp.bfloat16)
        partial_logit = jnp.sum(layer_out.astype(jnp.float32) * head_weight[None, :], axis=1)
        inputs_all = keep_slot(inputs_all, whole_rows, micro_slot, is_live)
        pre_all = keep_slot(pre_all, pre_act, micro_slot, is_live)
        logits_all = keep_slot(
            logits_all, partial_logit, micro_slot, is_live & (section_index == sections - 1)
        )
        incoming = shifted(layer_out, "section", 1)
        return (incoming, inputs_all, pre_all, logits_all, spectral, new_u)

    start_state = (
        jnp.zeros((batch_rows, local_cols), jnp.bfloat16),
        jnp.zeros((micro_count, batch_rows, full_width), jnp.bfloat16),
        jnp.zeros((micro_count, batch_rows, local_cols), jnp.float32),
        jnp.zeros((micro_count, batch_rows), jnp.float32),
        spectral_init,
        new_init,
    )
    _, inputs_all, pre_all, partial_logits, spectral, new_u = lax.fori_loop(
        0, tick_count, forward_tick, start_state
    )
    logits_all = by_axis(partial_logits, MP)

    def backward_tick(tick_now, state_all):
        incoming, grad_all = state_all
        micro_index = tick_now - (sections - 1 - section_index)
        is_live = (micro_index >= 0) & (micro_index < micro_count)
        micro_slot = jnp.clip(micro_index, 0, micro_count - 1)
        sign_row = lax.dynamic_index_in_dim(sign_all, micro_slot, 0, keepdims=False)
        logit_row = lax.dynamic_index_in_dim(logits_all, micro_slot, 0, keepdims=False)
        top_scale = -loss_scale * sign_row * jax.nn.sigmoid(-sign_row * logit_row)
        top_grad = (top_scale[:, None] * head_weight[None, :]).astype(jnp.bfloat16)
        grad_out = jnp.where(section_index == sections - 1, top_grad, incoming)
        pre_act = lax.dynamic_index_in_dim(pre_all, micro_slot, 0, keepdims=False)
        grad_pre = (grad_out.astype(jnp.float32) * silu_slope(pre_act)).astype(jnp.bfloat16)
        partial_term = lax.dot_general(
            grad_pre, weight, (((1,), (1,)), ((), ())), preferred_element_type=jnp.float32
        )
        received = lax.all_to_all(
            partial_term.astype(jnp.bfloat16), MP, split_axis=1, concat_axis=0, tiled=True
        ).astype(partial_term.dtype)
        back_sum = jnp.sum(received.reshape(-1, batch_rows, local_cols), axis=0)
        grad_in = (grad_out.astype(jnp.float32) + back_sum / spectral).astype(jnp.bfloat16)
        grad_all = keep_slot(grad_all, grad_pre, micro_slot, is_live)
        incoming = shifted(grad_in, "section", -1)
        return (incoming, grad_all)

    back_state = (
        jnp.zeros((batch_rows, local_cols), jnp.bfloat16),
        jnp.zeros((micro_count, batch_rows, local_cols), jnp.bfloat16),
    )
    _, grad_all = lax.fori_loop(0, tick_count, backward_tick, back_state)
    whole_rows = inputs_all.reshape(micro_count * batch_rows, full_width)
    grad_rows = grad_all.reshape(micro_count * batch_rows, local_cols)
    outer_sum = lax.dot_general(
        whole_rows, grad_rows, (((0,), (0,)), ((), ())), preferred_element_type=jnp.float32
    )
    weight_grad = (outer_sum / spectral).astype(jnp.bfloat16)
    inner_total = by_axis(jnp.sum(outer_sum * weight.astype(jnp.float32)), MP)
    rank_coef = inner_total / (spectral * spectral)
    return (weight_grad[None], new_u[None], rank_coef.reshape(1))


def solution(mesh):
    torus = Mesh(mesh.devices.reshape(mesh.shape["section"], 16, 4), ("section", "mp_0", "mp_1"))
    placed = (P(None, None, MP), P(), P("section", None, MP), P("section", MP), P(MP))
    return jax.shard_map(
        on_device,
        mesh=torus,
        in_specs=placed,
        out_specs=(P("section", None, MP), P("section", MP), P("section")),
        check_vma=False,
    )
```

profile of v0, /device:TPU:8, one launch (start us, length us, event | category | flops | bytes accessed | tf_op | source)
XLA Modules:
  0.0 1187.2 jit_solution(8960027373483992137)
XLA Ops:
  3.0 62.0 %psum.56 = f32[8192]{0:T(1024)S(1)} all-reduce(f32[8192]{0:T(1024)S(1)} %bitcast.117), channel_id=1, replica_groups=mesh['section'=8,'mp_0'=16,'mp_1'=4] {'mp_0'}, use_global_device_ids=true, to_apply=%region_0.0 | all-reduce | flops 8192 | bytes 65536 | tf_op jit(solution)/shard_map/psum | solution.py:17
  65.1 17.1 %psum.57 = f32[8192]{0:T(1024)S(1)} all-reduce(f32[8192]{0:T(1024)S(1)} %psum.56), channel_id=1, replica_groups=mesh['section'=8,'mp_0'=16,'mp_1'=4] {'mp_1'}, use_global_device_ids=true, to_apply=%region_1.0 | all-reduce | flops 8192 | bytes 65536 | tf_op jit(solution)/shard_map/psum | solution.py:17
  84.5 28.7 %psum.58 = f32[]{:T(128)} all-reduce(f32[]{:T(128)} %get-tuple-element.515), channel_id=1, replica_groups=mesh['section'=8,'mp_0'=16,'mp_1'=4] {'mp_0'}, use_global_device_ids=true, to_apply=%region_4.0 | all-reduce | flops 1 | bytes 8 | tf_op jit(solution)/shard_map/psum | solution.py:17
  123.9 498.0 %while.37 = (s32[]{:T(128)}, bf16[32,128]{1,0:T(8,128)(2,1)S(1)}, bf16[4,32,8192]{2,1,0:T(8,128)(2,1)}, f32[4,32,128]{2,1,0:T(8,128)S(1)}, f32[4,32]{1,0:T(4,128...) while((s32[]{:T(128)}, bf16[32,128]{1,0:T(8,128)(2,1)S(1)}, ...), condition=%wide.region_8.9_spmd, body=%wide.region_6.8_spmd.sunk | while | flops 67424256 | bytes 10667605 | solution.py:107
  125.5 8.7 all-to-all-start
  134.2 23.0 %all-to-all-done = bf16[64,32,128]{2,1,0:T(8,128)(2,1)S(1)} async-done(((bf16[64,32,128]{2,1,0:T(8,128)(2,1)}), bf16[64,32,128]{2,1,0:T(8,128)(2,1)S(1)}, u32[]{:S(2)}, u32[]{:S(2)}) %all-to-all-start) | async-done | bytes 524320 | tf_op jit(solution)/shard_map/while/body/eval_jaxpr/all_to_all | solution.py:22
  171.4 33.6 %all-to-all-done = bf16[64,32,128]{2,1,0:T(8,128)(2,1)S(1)} async-done(((bf16[64,32,128]{2,1,0:T(8,128)(2,1)}), bf16[64,32,128]{2,1,0:T(8,128)(2,1)S(1)}, u32[]{:S(2)}, u32[]{:S(2)}) %all-to-all-start) | async-done | bytes 524320 | tf_op jit(solution)/shard_map/while/body/eval_jaxpr/all_to_all | solution.py:22
  219.2 33.3 %all-to-all-done = bf16[64,32,128]{2,1,0:T(8,128)(2,1)S(1)} async-done(((bf16[64,32,128]{2,1,0:T(8,128)(2,1)}), bf16[64,32,128]{2,1,0:T(8,128)(2,1)S(1)}, u32[]{:S(2)}, u32[]{:S(2)}) %all-to-all-start) | async-done | bytes 524320 | tf_op jit(solution)/shard_map/while/body/eval_jaxpr/all_to_all | solution.py:22
  266.8 31.5 %all-to-all-done = bf16[64,32,128]{2,1,0:T(8,128)(2,1)S(1)} async-done(((bf16[64,32,128]{2,1,0:T(8,128)(2,1)}), bf16[64,32,128]{2,1,0:T(8,128)(2,1)S(1)}, u32[]{:S(2)}, u32[]{:S(2)}) %all-to-all-start) | async-done | bytes 524320 | tf_op jit(solution)/shard_map/while/body/eval_jaxpr/all_to_all | solution.py:22
  312.3 31.4 %all-to-all-done = bf16[64,32,128]{2,1,0:T(8,128)(2,1)S(1)} async-done(((bf16[64,32,128]{2,1,0:T(8,128)(2,1)}), bf16[64,32,128]{2,1,0:T(8,128)(2,1)S(1)}, u32[]{:S(2)}, u32[]{:S(2)}) %all-to-all-start) | async-done | bytes 524320 | tf_op jit(solution)/shard_map/while/body/eval_jaxpr/all_to_all | solution.py:22
  358.0 30.7 %all-to-all-done = bf16[64,32,128]{2,1,0:T(8,128)(2,1)S(1)} async-done(((bf16[64,32,128]{2,1,0:T(8,128)(2,1)}), bf16[64,32,128]{2,1,0:T(8,128)(2,1)S(1)}, u32[]{:S(2)}, u32[]{:S(2)}) %all-to-all-start) | async-done | bytes 524320 | tf_op jit(solution)/shard_map/while/body/eval_jaxpr/all_to_all | solution.py:22
  403.3 30.8 %all-to-all-done = bf16[64,32,128]{2,1,0:T(8,128)(2,1)S(1)} async-done(((bf16[64,32,128]{2,1,0:T(8,128)(2,1)}), bf16[64,32,128]{2,1,0:T(8,128)(2,1)S(1)}, u32[]{:S(2)}, u32[]{:S(2)}) %all-to-all-start) | async-done | bytes 524320 | tf_op jit(solution)/shard_map/while/body/eval_jaxpr/all_to_all | solution.py:22
  448.5 30.8 %all-to-all-done = bf16[64,32,128]{2,1,0:T(8,128)(2,1)S(1)} async-done(((bf16[64,32,128]{2,1,0:T(8,128)(2,1)}), bf16[64,32,128]{2,1,0:T(8,128)(2,1)S(1)}, u32[]{:S(2)}, u32[]{:S(2)}) %all-to-all-start) | async-done | bytes 524320 | tf_op jit(solution)/shard_map/while/body/eval_jaxpr/all_to_all | solution.py:22
  493.8 30.8 %all-to-all-done = bf16[64,32,128]{2,1,0:T(8,128)(2,1)S(1)} async-done(((bf16[64,32,128]{2,1,0:T(8,128)(2,1)}), bf16[64,32,128]{2,1,0:T(8,128)(2,1)S(1)}, u32[]{:S(2)}, u32[]{:S(2)}) %all-to-all-start) | async-done | bytes 524320 | tf_op jit(solution)/shard_map/while/body/eval_jaxpr/all_to_all | solution.py:22
  539.0 30.8 %all-to-all-done = bf16[64,32,128]{2,1,0:T(8,128)(2,1)S(1)} async-done(((bf16[64,32,128]{2,1,0:T(8,128)(2,1)}), bf16[64,32,128]{2,1,0:T(8,128)(2,1)S(1)}, u32[]{:S(2)}, u32[]{:S(2)}) %all-to-all-start) | async-done | bytes 524320 | tf_op jit(solution)/shard_map/while/body/eval_jaxpr/all_to_all | solution.py:22
  584.3 30.8 %all-to-all-done = bf16[64,32,128]{2,1,0:T(8,128)(2,1)S(1)} async-done(((bf16[64,32,128]{2,1,0:T(8,128)(2,1)}), bf16[64,32,128]{2,1,0:T(8,128)(2,1)S(1)}, u32[]{:S(2)}, u32[]{:S(2)}) %all-to-all-start) | async-done | bytes 524320 | tf_op jit(solution)/shard_map/while/body/eval_jaxpr/all_to_all | solution.py:22
  621.8 27.3 %psum.60 = f32[4,32]{1,0:T(4,128)S(1)} all-reduce(f32[4,32]{1,0:T(4,128)S(1)} %get-tuple-element.461), channel_id=1, replica_groups=mesh['section'=8,'mp_0'=16,'mp_1'=4] {'mp_0'}, use_global_device_ids=true, to_apply=%region_9.10 | all-reduce | flops 128 | bytes 1024 | tf_op jit(solution)/shard_map/psum | solution.py:17
  649.1 10.4 psum.61
  659.6 481.5 %while.38 = (s32[]{:T(128)}, bf16[32,128]{1,0:T(8,128)(2,1)S(1)}, bf16[4,32,128]{2,1,0:T(8,128)(2,1)S(1)}, pred[]{:T(512)}, s32[]{:T(128)}, /*index=5*/f32[4,32]...) while((s32[]{:T(128)}, bf16[32,128]{1,0:T(8,128)(2,1)S(1)}, ...), condition=%wide.region_13.14_spmd, body=%wide.region_11.13_spmd.sunk | while | flops 68030688 | bytes 5950758 | solution.py:140
  667.5 23.0 %all-to-all-done.1 = bf16[32,64,128]{2,0,1:T(8,128)(2,1)S(1)} async-done(((bf16[32,64,128]{2,0,1:T(8,128)(2,1)}), bf16[32,64,128]{2,0,1:T(8,128)(2,1)S(1)}, u32[]{:S(2)}, u32[]{:S(2)}) %all-to-all-start.1) | async-done | bytes 524320 | tf_op jit(solution)/shard_map/while/body/eval_jaxpr/all_to_all | solution.py:127
  701.4 32.9 %all-to-all-done.1 = bf16[32,64,128]{2,0,1:T(8,128)(2,1)S(1)} async-done(((bf16[32,64,128]{2,0,1:T(8,128)(2,1)}), bf16[32,64,128]{2,0,1:T(8,128)(2,1)S(1)}, u32[]{:S(2)}, u32[]{:S(2)}) %all-to-all-start.1) | async-done | bytes 524320 | tf_op jit(solution)/shard_map/while/body/eval_jaxpr/all_to_all | solution.py:127
  746.7 32.3 %all-to-all-done.1 = bf16[32,64,128]{2,0,1:T(8,128)(2,1)S(1)} async-done(((bf16[32,64,128]{2,0,1:T(8,128)(2,1)}), bf16[32,64,128]{2,0,1:T(8,128)(2,1)S(1)}, u32[]{:S(2)}, u32[]{:S(2)}) %all-to-all-start.1) | async-done | bytes 524320 | tf_op jit(solution)/shard_map/while/body/eval_jaxpr/all_to_all | solution.py:127
  792.4 31.6 %all-to-all-done.1 = bf16[32,64,128]{2,0,1:T(8,128)(2,1)S(1)} async-done(((bf16[32,64,128]{2,0,1:T(8,128)(2,1)}), bf16[32,64,128]{2,0,1:T(8,128)(2,1)S(1)}, u32[]{:S(2)}, u32[]{:S(2)}) %all-to-all-start.1) | async-done | bytes 524320 | tf_op jit(solution)/shard_map/while/body/eval_jaxpr/all_to_all | solution.py:127
  837.2 31.5 %all-to-all-done.1 = bf16[32,64,128]{2,0,1:T(8,128)(2,1)S(1)} async-done(((bf16[32,64,128]{2,0,1:T(8,128)(2,1)}), bf16[32,64,128]{2,0,1:T(8,128)(2,1)S(1)}, u32[]{:S(2)}, u32[]{:S(2)}) %all-to-all-start.1) | async-done | bytes 524320 | tf_op jit(solution)/shard_map/while/body/eval_jaxpr/all_to_all | solution.py:127
  881.6 31.7 %all-to-all-done.1 = bf16[32,64,128]{2,0,1:T(8,128)(2,1)S(1)} async-done(((bf16[32,64,128]{2,0,1:T(8,128)(2,1)}), bf16[32,64,128]{2,0,1:T(8,128)(2,1)S(1)}, u32[]{:S(2)}, u32[]{:S(2)}) %all-to-all-start.1) | async-done | bytes 524320 | tf_op jit(solution)/shard_map/while/body/eval_jaxpr/all_to_all | solution.py:127
  926.0 32.1 %all-to-all-done.1 = bf16[32,64,128]{2,0,1:T(8,128)(2,1)S(1)} async-done(((bf16[32,64,128]{2,0,1:T(8,128)(2,1)}), bf16[32,64,128]{2,0,1:T(8,128)(2,1)S(1)}, u32[]{:S(2)}, u32[]{:S(2)}) %all-to-all-start.1) | async-done | bytes 524320 | tf_op jit(solution)/shard_map/while/body/eval_jaxpr/all_to_all | solution.py:127
  970.5 32.4 %all-to-all-done.1 = bf16[32,64,128]{2,0,1:T(8,128)(2,1)S(1)} async-done(((bf16[32,64,128]{2,0,1:T(8,128)(2,1)}), bf16[32,64,128]{2,0,1:T(8,128)(2,1)S(1)}, u32[]{:S(2)}, u32[]{:S(2)}) %all-to-all-start.1) | async-done | bytes 524320 | tf_op jit(solution)/shard_map/while/body/eval_jaxpr/all_to_all | solution.py:127
  1014.9 32.8 %all-to-all-done.1 = bf16[32,64,128]{2,0,1:T(8,128)(2,1)S(1)} async-done(((bf16[32,64,128]{2,0,1:T(8,128)(2,1)}), bf16[32,64,128]{2,0,1:T(8,128)(2,1)S(1)}, u32[]{:S(2)}, u32[]{:S(2)}) %all-to-all-start.1) | async-done | bytes 524320 | tf_op jit(solution)/shard_map/while/body/eval_jaxpr/all_to_all | solution.py:127
  1059.3 33.2 %all-to-all-done.1 = bf16[32,64,128]{2,0,1:T(8,128)(2,1)S(1)} async-done(((bf16[32,64,128]{2,0,1:T(8,128)(2,1)}), bf16[32,64,128]{2,0,1:T(8,128)(2,1)S(1)}, u32[]{:S(2)}, u32[]{:S(2)}) %all-to-all-start.1) | async-done | bytes 524320 | tf_op jit(solution)/shard_map/while/body/eval_jaxpr/all_to_all | solution.py:127
  1103.7 33.9 %all-to-all-done.1 = bf16[32,64,128]{2,0,1:T(8,128)(2,1)S(1)} async-done(((bf16[32,64,128]{2,0,1:T(8,128)(2,1)}), bf16[32,64,128]{2,0,1:T(8,128)(2,1)S(1)}, u32[]{:S(2)}, u32[]{:S(2)}) %all-to-all-start.1) | async-done | bytes 524320 | tf_op jit(solution)/shard_map/while/body/eval_jaxpr/all_to_all | solution.py:127
  1145.8 28.0 %psum.62 = f32[]{:T(128)} all-reduce(f32[]{:T(128)} %get-tuple-element.513), channel_id=1, replica_groups=mesh['section'=8,'mp_0'=16,'mp_1'=4] {'mp_0'}, use_global_device_ids=true, to_apply=%region_15.16 | all-reduce | flops 1 | bytes 8 | tf_op jit(solution)/shard_map/psum | solution.py:17
  1173.8 11.1 psum.63
  (306 shorter events, 303.9 us)
Async XLA Ops:
  125.5 31.7 %all-to-all-start = ((bf16[64,32,128]{2,1,0:T(8,128)(2,1)}), bf16[64,32,128]{2,1,0:T(8,128)(2,1)S(1)}, u32[]{:S(2)}, u32[]{:S(2)}) async-start(bf16[64,32,128]{2,1,0:T(8,128)(2,1)} %broadcast_in_dim.78), calls=%async_computation | async-start | bytes 1048576 | tf_op jit(solution)/shard_map/while/body/eval_jaxpr/all_to_all | solution.py:22
  159.0 5.0 collective-permute-start
  165.5 39.5 %all-to-all-start = ((bf16[64,32,128]{2,1,0:T(8,128)(2,1)}), bf16[64,32,128]{2,1,0:T(8,128)(2,1)S(1)}, u32[]{:S(2)}, u32[]{:S(2)}) async-start(bf16[64,32,128]{2,1,0:T(8,128)(2,1)} %broadcast_in_dim.78), calls=%async_computation | async-start | bytes 1048576 | tf_op jit(solution)/shard_map/while/body/eval_jaxpr/all_to_all | solution.py:22
  206.8 5.0 collective-permute-start
  213.4 39.2 %all-to-all-start = ((bf16[64,32,128]{2,1,0:T(8,128)(2,1)}), bf16[64,32,128]{2,1,0:T(8,128)(2,1)S(1)}, u32[]{:S(2)}, u32[]{:S(2)}) async-start(bf16[64,32,128]{2,1,0:T(8,128)(2,1)} %broadcast_in_dim.78), calls=%async_computation | async-start | bytes 1048576 | tf_op jit(solution)/shard_map/while/body/eval_jaxpr/all_to_all | solution.py:22
  254.4 5.0 collective-permute-start
  260.9 37.4 %all-to-all-start = ((bf16[64,32,128]{2,1,0:T(8,128)(2,1)}), bf16[64,32,128]{2,1,0:T(8,128)(2,1)S(1)}, u32[]{:S(2)}, u32[]{:S(2)}) async-start(bf16[64,32,128]{2,1,0:T(8,128)(2,1)} %broadcast_in_dim.78), calls=%async_computation | async-start | bytes 1048576 | tf_op jit(solution)/shard_map/while/body/eval_jaxpr/all_to_all | solution.py:22
  300.1 5.0 collective-permute-start
  306.6 37.1 %all-to-all-start = ((bf16[64,32,128]{2,1,0:T(8,128)(2,1)}), bf16[64,32,128]{2,1,0:T(8,128)(2,1)S(1)}, u32[]{:S(2)}, u32[]{:S(2)}) async-start(bf16[64,32,128]{2,1,0:T(8,128)(2,1)} %broadcast_in_dim.78), calls=%async_computation | async-start | bytes 1048576 | tf_op jit(solution)/shard_map/while/body/eval_jaxpr/all_to_all | solution.py:22
  345.4 5.1 collective-permute-start
  352.2 36.6 %all-to-all-start = ((bf16[64,32,128]{2,1,0:T(8,128)(2,1)}), bf16[64,32,128]{2,1,0:T(8,128)(2,1)S(1)}, u32[]{:S(2)}, u32[]{:S(2)}) async-start(bf16[64,32,128]{2,1,0:T(8,128)(2,1)} %broadcast_in_dim.78), calls=%async_computation | async-start | bytes 1048576 | tf_op jit(solution)/shard_map/while/body/eval_jaxpr/all_to_all | solution.py:22
  390.5 5.0 collective-permute-start
  397.1 36.9 %all-to-all-start = ((bf16[64,32,128]{2,1,0:T(8,128)(2,1)}), bf16[64,32,128]{2,1,0:T(8,128)(2,1)S(1)}, u32[]{:S(2)}, u32[]{:S(2)}) async-start(bf16[64,32,128]{2,1,0:T(8,128)(2,1)} %broadcast_in_dim.78), calls=%async_computation | async-start | bytes 1048576 | tf_op jit(solution)/shard_map/while/body/eval_jaxpr/all_to_all | solution.py:22
  435.8 5.0 collective-permute-start
  442.3 36.9 %all-to-all-start = ((bf16[64,32,128]{2,1,0:T(8,128)(2,1)}), bf16[64,32,128]{2,1,0:T(8,128)(2,1)S(1)}, u32[]{:S(2)}, u32[]{:S(2)}) async-start(bf16[64,32,128]{2,1,0:T(8,128)(2,1)} %broadcast_in_dim.78), calls=%async_computation | async-start | bytes 1048576 | tf_op jit(solution)/shard_map/while/body/eval_jaxpr/all_to_all | solution.py:22
  487.6 36.9 %all-to-all-start = ((bf16[64,32,128]{2,1,0:T(8,128)(2,1)}), bf16[64,32,128]{2,1,0:T(8,128)(2,1)S(1)}, u32[]{:S(2)}, u32[]{:S(2)}) async-start(bf16[64,32,128]{2,1,0:T(8,128)(2,1)} %broadcast_in_dim.78), calls=%async_computation | async-start | bytes 1048576 | tf_op jit(solution)/shard_map/while/body/eval_jaxpr/all_to_all | solution.py:22
  532.9 36.9 %all-to-all-start = ((bf16[64,32,128]{2,1,0:T(8,128)(2,1)}), bf16[64,32,128]{2,1,0:T(8,128)(2,1)S(1)}, u32[]{:S(2)}, u32[]{:S(2)}) async-start(bf16[64,32,128]{2,1,0:T(8,128)(2,1)} %broadcast_in_dim.78), calls=%async_computation | async-start | bytes 1048576 | tf_op jit(solution)/shard_map/while/body/eval_jaxpr/all_to_all | solution.py:22
  578.1 36.9 %all-to-all-start = ((bf16[64,32,128]{2,1,0:T(8,128)(2,1)}), bf16[64,32,128]{2,1,0:T(8,128)(2,1)S(1)}, u32[]{:S(2)}, u32[]{:S(2)}) async-start(bf16[64,32,128]{2,1,0:T(8,128)(2,1)} %broadcast_in_dim.78), calls=%async_computation | async-start | bytes 1048576 | tf_op jit(solution)/shard_map/while/body/eval_jaxpr/all_to_all | solution.py:22
  661.4 29.1 %all-to-all-start.1 = ((bf16[32,64,128]{2,0,1:T(8,128)(2,1)}), bf16[32,64,128]{2,0,1:T(8,128)(2,1)S(1)}, u32[]{:S(2)}, u32[]{:S(2)}) async-start(bf16[32,64,128]{2,0,1:T(8,128)(2,1)} %bitcast.113), calls=%async_computation.1 | async-start | bytes 1048576 | tf_op jit(solution)/shard_map/while/body/eval_jaxpr/all_to_all | solution.py:127
  695.7 38.6 %all-to-all-start.1 = ((bf16[32,64,128]{2,0,1:T(8,128)(2,1)}), bf16[32,64,128]{2,0,1:T(8,128)(2,1)S(1)}, u32[]{:S(2)}, u32[]{:S(2)}) async-start(bf16[32,64,128]{2,0,1:T(8,128)(2,1)} %bitcast.113), calls=%async_computation.1 | async-start | bytes 1048576 | tf_op jit(solution)/shard_map/while/body/eval_jaxpr/all_to_all | solution.py:127
  739.5 39.5 %all-to-all-start.1 = ((bf16[32,64,128]{2,0,1:T(8,128)(2,1)}), bf16[32,64,128]{2,0,1:T(8,128)(2,1)S(1)}, u32[]{:S(2)}, u32[]{:S(2)}) async-start(bf16[32,64,128]{2,0,1:T(8,128)(2,1)} %bitcast.113), calls=%async_computation.1 | async-start | bytes 1048576 | tf_op jit(solution)/shard_map/while/body/eval_jaxpr/all_to_all | solution.py:127
  779.2 5.7 collective-permute-start.1
  786.7 37.3 %all-to-all-start.1 = ((bf16[32,64,128]{2,0,1:T(8,128)(2,1)}), bf16[32,64,128]{2,0,1:T(8,128)(2,1)S(1)}, u32[]{:S(2)}, u32[]{:S(2)}) async-start(bf16[32,64,128]{2,0,1:T(8,128)(2,1)} %bitcast.113), calls=%async_computation.1 | async-start | bytes 1048576 | tf_op jit(solution)/shard_map/while/body/eval_jaxpr/all_to_all | solution.py:127
  824.2 5.4 collective-permute-start.1
  831.3 37.4 %all-to-all-start.1 = ((bf16[32,64,128]{2,0,1:T(8,128)(2,1)}), bf16[32,64,128]{2,0,1:T(8,128)(2,1)S(1)}, u32[]{:S(2)}, u32[]{:S(2)}) async-start(bf16[32,64,128]{2,0,1:T(8,128)(2,1)} %bitcast.113), calls=%async_computation.1 | async-start | bytes 1048576 | tf_op jit(solution)/shard_map/while/body/eval_jaxpr/all_to_all | solution.py:127
  868.9 5.1 collective-permute-start.1
  875.7 37.6 %all-to-all-start.1 = ((bf16[32,64,128]{2,0,1:T(8,128)(2,1)}), bf16[32,64,128]{2,0,1:T(8,128)(2,1)S(1)}, u32[]{:S(2)}, u32[]{:S(2)}) async-start(bf16[32,64,128]{2,0,1:T(8,128)(2,1)} %bitcast.113), calls=%async_computation.1 | async-start | bytes 1048576 | tf_op jit(solution)/shard_map/while/body/eval_jaxpr/all_to_all | solution.py:127
  920.2 37.9 %all-to-all-start.1 = ((bf16[32,64,128]{2,0,1:T(8,128)(2,1)}), bf16[32,64,128]{2,0,1:T(8,128)(2,1)S(1)}, u32[]{:S(2)}, u32[]{:S(2)}) async-start(bf16[32,64,128]{2,0,1:T(8,128)(2,1)} %bitcast.113), calls=%async_computation.1 | async-start | bytes 1048576 | tf_op jit(solution)/shard_map/while/body/eval_jaxpr/all_to_all | solution.py:127
  964.6 38.3 %all-to-all-start.1 = ((bf16[32,64,128]{2,0,1:T(8,128)(2,1)}), bf16[32,64,128]{2,0,1:T(8,128)(2,1)S(1)}, u32[]{:S(2)}, u32[]{:S(2)}) async-start(bf16[32,64,128]{2,0,1:T(8,128)(2,1)} %bitcast.113), calls=%async_computation.1 | async-start | bytes 1048576 | tf_op jit(solution)/shard_map/while/body/eval_jaxpr/all_to_all | solution.py:127
  1009.0 38.7 %all-to-all-start.1 = ((bf16[32,64,128]{2,0,1:T(8,128)(2,1)}), bf16[32,64,128]{2,0,1:T(8,128)(2,1)S(1)}, u32[]{:S(2)}, u32[]{:S(2)}) async-start(bf16[32,64,128]{2,0,1:T(8,128)(2,1)} %bitcast.113), calls=%async_computation.1 | async-start | bytes 1048576 | tf_op jit(solution)/shard_map/while/body/eval_jaxpr/all_to_all | solution.py:127
  1053.4 39.1 %all-to-all-start.1 = ((bf16[32,64,128]{2,0,1:T(8,128)(2,1)}), bf16[32,64,128]{2,0,1:T(8,128)(2,1)S(1)}, u32[]{:S(2)}, u32[]{:S(2)}) async-start(bf16[32,64,128]{2,0,1:T(8,128)(2,1)} %bitcast.113), calls=%async_computation.1 | async-start | bytes 1048576 | tf_op jit(solution)/shard_map/while/body/eval_jaxpr/all_to_all | solution.py:127
  1097.8 39.8 %all-to-all-start.1 = ((bf16[32,64,128]{2,0,1:T(8,128)(2,1)}), bf16[32,64,128]{2,0,1:T(8,128)(2,1)S(1)}, u32[]{:S(2)}, u32[]{:S(2)}) async-start(bf16[32,64,128]{2,0,1:T(8,128)(2,1)} %bitcast.113), calls=%async_computation.1 | async-start | bytes 1048576 | tf_op jit(solution)/shard_map/while/body/eval_jaxpr/all_to_all | solution.py:127
  (26 other events, 736.9 us)
where the time goes:
time: 1190 us
  waiting for transfers between devices  710 us (60%)
  blocking collectives  193 us (16%)
  starting transfers between devices  187 us (16%)
  local copies, waits for them, and re-layouts  35.1 us (3%)
  other arithmetic  33.7 us (3%)
  matrix products  23.8 us (2%)
    all_to_all x11, waiting for transfers between devices, backward_tick(): lax.all_to_all(partial_term.astype(jnp.bfloat16), MP, split_axis=1, conca...  348 us
    all_to_all x11, waiting for transfers between devices, from_everyone(): lax.all_to_all(jnp.broadcast_to(shard[None], (devices, *shard.shape)), ax...  337 us
    psum x8, blocking collectives, by_axis(): return functools.reduce(lax.psum, axes, shard)  193 us
    all_to_all x11, starting transfers between devices, from_everyone(): lax.all_to_all(jnp.broadcast_to(shard[None], (devices, *shard.shape)), ax...  68.3 us
    all_to_all x11, starting transfers between devices, backward_tick(): lax.all_to_all(partial_term.astype(jnp.bfloat16), MP, split_axis=1, conca...  65.4 us
    ppermute x22, starting transfers between devices, shifted(): return lax.ppermute(block, axis, route)  52.8 us
    ppermute x22, waiting for transfers between devices, shifted(): return lax.ppermute(block, axis, route)  25.1 us
  transfers between devices with their start and end apart: 44, of which 44 were waited for; matrix products, arithmetic and copies ran while one was open for 2% of the time, Pallas kernels for 0%

commit v1 on v0

v1 whole, which is shorter than its diff:
```python
import functools

import jax
import jax.numpy as jnp
from jax import lax
from jax.experimental import pallas as pl
from jax.experimental.pallas import tpu as pltpu
from jax.sharding import Mesh
from jax.sharding import PartitionSpec as P

MP = ("mp_0", "mp_1")
loss_scale = 32.0
tiny_eps = 1e-06
LANES = 128


def silu_slope(pre_act):
    gate_val = jax.nn.sigmoid(pre_act)
    return gate_val * (1.0 + pre_act * (1.0 - gate_val))


def far_first(count):
    return sorted(range(count), key=lambda d: -min(d, count - d))


def remote(src, dst, send, recv, device):
    return pltpu.make_async_remote_copy(
        src_ref=src,
        dst_ref=dst,
        send_sem=send,
        recv_sem=recv,
        device_id=device,
        device_id_type=pl.DeviceIdType.MESH,
    )


def await_bytes(ref, sem):
    pltpu.make_async_copy(ref, ref, sem).wait()


def step_kernel(
    dims,
    feat,
    labels,
    w,
    u,
    head,
    wg_out,
    nu_out,
    coef_out,
    hid,
    hout,
    pre,
    gpre,
    ghid,
    part,
    part_in,
    colsum,
    col_in,
    gh_in,
    left_x,
    left_xin,
    left_z,
    left_zin,
    left_all,
    norm_z,
    norm_x,
    logit_z,
    logit_x,
    coef_z,
    coef_x,
    inv_sig,
    small_send,
    small_recv,
    fz_send,
    fz_recv,
    fx_send,
    fx_recv,
    bx_send,
    bx_recv,
    bz_send,
    bz_recv,
    bg_send,
    bg_recv,
    lz_send,
    lz_recv,
    lx_send,
    lx_recv,
):
    S, Z, X, n, R = dims
    s = lax.axis_index("section")
    z = lax.axis_index("mp_0")
    x = lax.axis_index("mp_1")
    nxt = lax.rem(s + 1, S)
    prv = lax.rem(s + S - 1, S)
    z_far = far_first(Z)

    def zat(d):
        return lax.rem(z + d, Z)

    def xat(d):
        return lax.rem(x + d, X)

    barrier = pltpu.get_barrier_semaphore()

    def greet(device):
        pl.semaphore_signal(
            barrier, inc=1, device_id=device, device_id_type=pl.DeviceIdType.MESH
        )

    for d in z_far:
        greet((nxt, zat(d), x))
        greet((prv, zat(d), x))
        if d:
            greet((s, zat(d), x))
    for d in range(1, X):
        greet((s, z, xat(d)))

    u_rows = jnp.broadcast_to(u[...], (16, LANES)).astype(jnp.bfloat16)

    def left_block(zi, carry):
        for xi in range(X):
            block = lax.dot_general(
                u_rows, w[zi * X + xi], (((1,), (1,)), ((), ())),
                preferred_element_type=jnp.float32,
            )
            left_x[xi, zi] = block[0:1]
        return carry

    lax.fori_loop(0, Z, left_block, 0)
    pl.semaphore_wait(barrier, 3 * Z - 1 + X - 1)

    @pl.when(s == S - 1)
    def _():
        def send_features(m, carry):
            for d in z_far:
                remote(
                    feat.at[m], hid.at[m, x, z], fz_send.at[m], fz_recv.at[m], (nxt, zat(d), x)
                ).start()
            return carry

        lax.fori_loop(0, n, send_features, 0)

    def spread_z(src, dst, k):
        for d in z_far:
            if d:
                remote(src(d), dst, small_send.at[k], small_recv.at[k], (s, zat(d), x)).start()

    def spread_x(src, dst, k):
        for d in range(1, X):
            remote(src(d), dst, small_send.at[k], small_recv.at[k], (s, z, xat(d))).start()

    spread_x(lambda d: left_x.at[xat(d)], left_xin.at[x], 0)
    await_bytes(left_xin.at[pl.ds(0, X - 1)], small_recv.at[0])
    column = left_x[x]
    for d in range(1, X):
        column = column + left_xin[xat(d)]
    left_z[...] = column
    spread_z(lambda d: left_z.at[zat(d)], left_zin.at[z], 1)
    await_bytes(left_zin.at[pl.ds(0, Z - 1)], small_recv.at[1])
    left_zin[z] = left_z[z]
    left_all[x, z] = jnp.sum(left_zin[...], axis=0)
    spread_z(lambda d: left_all.at[x, z], left_all.at[x, z], 2)

    def forward_columns(m):
        await_bytes(hid.at[m, x], fz_recv.at[m])
        for d in range(1, X):
            remote(
                hid.at[m, x], hid.at[m, x], fx_send.at[m], fx_recv.at[m, x], (s, z, xat(d))
            ).start()

    @pl.when(s == 0)
    def _():
        def pass_on(m, carry):
            forward_columns(m)
            return carry

        lax.fori_loop(0, n, pass_on, 0)

    await_bytes(left_all.at[0, pl.ds(0, Z - 1)], small_recv.at[2])
    spread_x(lambda d: left_all.at[x], left_all.at[x], 3)
    await_bytes(left_all.at[pl.ds(0, X - 1)], small_recv.at[3])

    left = left_all[...]
    total = jnp.sum(jnp.sum(left * left, axis=(0, 1)), axis=-1, keepdims=True)
    scale_v = lax.rsqrt(total + tiny_eps)

    def pair(ref_rows):
        return jnp.concatenate(ref_rows, axis=1)

    def w_pair(xi, zi):
        return jnp.concatenate([w[zi * X + xi], w[(zi + 1) * X + xi]], axis=0)

    def right_block(zp, acc):
        zi = zp * 2
        for xi in range(X):
            rows = [
                jnp.broadcast_to(left_all[xi, zi + k] * scale_v, (16, LANES)).astype(jnp.bfloat16)
                for k in range(2)
            ]
            acc = acc + jnp.dot(pair(rows), w_pair(xi, zi), preferred_element_type=jnp.float32)
        return acc

    right = lax.fori_loop(0, Z // 2, right_block, jnp.zeros((16, LANES), jnp.float32))[0:1]

    def all_sum(value, zbuf, xbuf, kz, kx):
        zbuf[z] = value
        spread_z(lambda d: zbuf.at[z], zbuf.at[z], kz)
        await_bytes(zbuf.at[pl.ds(0, Z - 1)], small_recv.at[kz])
        xbuf[x] = jnp.sum(zbuf[...], axis=0)
        spread_x(lambda d: xbuf.at[x], xbuf.at[x], kx)
        await_bytes(xbuf.at[pl.ds(0, X - 1)], small_recv.at[kx])
        return jnp.sum(jnp.sum(xbuf[...], axis=0), axis=-1, keepdims=True)

    norm_total = all_sum(right * right, norm_z, norm_x, 4, 5)
    inv = 1.0 / jnp.sqrt(norm_total + tiny_eps)
    inv_sig[...] = jnp.broadcast_to(inv, (1, LANES))
    nu_out[...] = right * inv

    def forward_micro(m, carry):
        @pl.when(s > 0)
        def _():
            forward_columns(m)

        acc = jnp.zeros((R, LANES), jnp.float32)
        for d in range(X):
            xi = xat(d)
            if d:
                await_bytes(hid.at[m, xi], fx_recv.at[m, xi])
            for zi in range(0, Z, 2):
                acc = acc + jnp.dot(
                    pair([hid[m, xi, zi], hid[m, xi, zi + 1]]), w_pair(xi, zi),
                    preferred_element_type=jnp.float32,
                )
        pre_act = acc * inv_sig[...]
        pre[m] = pre_act
        out = (hid[m, x, z].astype(jnp.float32) + pre_act * jax.nn.sigmoid(pre_act)).astype(
            jnp.bfloat16
        )
        hout[m] = out

        @pl.when(s < S - 1)
        def _():
            for d in z_far:
                remote(
                    hout.at[m], hid.at[m, x, z], fz_send.at[m], fz_recv.at[m], (nxt, zat(d), x)
                ).start()

        @pl.when(s == S - 1)
        def _():
            terms = jnp.sum(out.astype(jnp.float32) * head[...], axis=1, keepdims=True)
            lane = lax.broadcasted_iota(jnp.int32, (R, LANES), 1)
            row = lax.broadcasted_iota(jnp.int32, (R, LANES), 0)
            spread = jnp.where(lane == row, jnp.broadcast_to(terms, (R, LANES)), 0.0)
            logit_z[m, z] = jnp.sum(spread, axis=0, keepdims=True)
            for d in z_far:
                if d:
                    remote(
                        logit_z.at[m, z], logit_z.at[m, z], lz_send.at[m], lz_recv.at[m],
                        (s, zat(d), x),
                    ).start()

        return carry

    lax.fori_loop(0, n, forward_micro, 0)

    def backward_micro(m, carry):
        @pl.when(s == S - 1)
        def _():
            await_bytes(logit_z.at[m, pl.ds(0, Z - 1)], lz_recv.at[m])
            logit_x[m, x] = jnp.sum(logit_z[m], axis=0)
            for d in range(1, X):
                remote(
                    logit_x.at[m, x], logit_x.at[m, x], lx_send.at[m], lx_recv.at[m],
                    (s, z, xat(d)),
                ).start()
            await_bytes(logit_x.at[m, pl.ds(0, X - 1)], lx_recv.at[m])
            logit_row = jnp.sum(logit_x[m], axis=0)
            lane = lax.broadcasted_iota(jnp.int32, (R, LANES), 1)
            row = lax.broadcasted_iota(jnp.int32, (R, LANES), 0)
            sign_row = (2 * labels[m] - 1).astype(jnp.float32)
            top_row = -loss_scale * sign_row * jax.nn.sigmoid(-sign_row * logit_row)
            top = jnp.sum(
                jnp.where(lane == row, jnp.broadcast_to(top_row, (R, LANES)), 0.0),
                axis=1, keepdims=True,
            )
            ghid[m] = (top * head[...]).astype(jnp.bfloat16)

        @pl.when(s < S - 1)
        def _():
            await_bytes(col_in.at[m], bz_recv.at[m])
            await_bytes(gh_in.at[m], bg_recv.at[m])
            back = jnp.sum(col_in[m].astype(jnp.float32), axis=0)
            ghid[m] = (gh_in[m].astype(jnp.float32) + back).astype(jnp.bfloat16)

        grad = (ghid[m].astype(jnp.float32) * silu_slope(pre[m])).astype(jnp.bfloat16)
        gpre[m] = grad

        @pl.when(s > 0)
        def _():
            remote(
                ghid.at[m], gh_in.at[m], bg_send.at[m], bg_recv.at[m], (prv, z, x)
            ).start()
            for d in [*range(1, X), 0]:
                xi = xat(d)
                for zi in range(Z):
                    part[m, xi, zi] = lax.dot_general(
                        grad, w[zi * X + xi], (((1,), (1,)), ((), ())),
                        preferred_element_type=jnp.float32,
                    ).astype(jnp.bfloat16)
                if d:
                    remote(
                        part.at[m, xi], part_in.at[m, x], bx_send.at[m], bx_recv.at[m],
                        (s, z, xi),
                    ).start()
            await_bytes(part_in.at[m, pl.ds(0, X - 1)], bx_recv.at[m])
            for d in z_far:
                zi = zat(d)
                column_sum = part[m, x, zi].astype(jnp.float32)
                for e in range(1, X):
                    column_sum = column_sum + part_in[m, xat(e), zi].astype(jnp.float32)
                colsum[m, zi] = (column_sum * inv_sig[...]).astype(jnp.bfloat16)
            for d in z_far:
                zi = zat(d)
                remote(
                    colsum.at[m, zi], col_in.at[m, z], bz_send.at[m], bz_recv.at[m], (prv, zi, x)
                ).start()

        return carry

    lax.fori_loop(0, n, backward_micro, 0)

    inner = jnp.sum(gpre[...].astype(jnp.float32) * pre[...], axis=0)
    coef_z[z] = jnp.sum(inner, axis=0, keepdims=True)
    spread_z(lambda d: coef_z.at[z], coef_z.at[z], 6)

    grads = gpre[...].reshape(n * R, LANES)

    def weight_block(zi, carry):
        for xi in range(X):
            rows = hid[:, xi, zi].reshape(n * R, LANES)
            block = lax.dot_general(
                rows, grads, (((0,), (0,)), ((), ())), preferred_element_type=jnp.float32
            )
            wg_out[zi * X + xi] = (block * inv_sig[...]).astype(jnp.bfloat16)
        return carry

    lax.fori_loop(0, Z, weight_block, 0)

    await_bytes(coef_z.at[pl.ds(0, Z - 1)], small_recv.at[6])
    coef_x[x] = jnp.sum(coef_z[...], axis=0)
    spread_x(lambda d: coef_x.at[x], coef_x.at[x], 7)
    await_bytes(coef_x.at[pl.ds(0, X - 1)], small_recv.at[7])
    inner_total = jnp.sum(jnp.sum(coef_x[...], axis=0), axis=-1, keepdims=True)
    coef_out[...] = inner_total * inv_sig[...]

    await_bytes(left_xin.at[pl.ds(0, X - 1)], small_send.at[0])
    await_bytes(left_zin.at[pl.ds(0, Z - 1)], small_send.at[1])
    await_bytes(left_zin.at[pl.ds(0, Z - 1)], small_send.at[2])
    await_bytes(left_xin.at[pl.ds(0, X - 1)], small_send.at[3])
    for k, buf in ((4, norm_z), (6, coef_z)):
        await_bytes(buf.at[pl.ds(0, Z - 1)], small_send.at[k])
    for k, buf in ((5, norm_x), (7, coef_x)):
        await_bytes(buf.at[pl.ds(0, X - 1)], small_send.at[k])

    def drain(m, carry):
        await_bytes(hid.at[m, 0], fz_send.at[m])
        await_bytes(hid.at[m, pl.ds(0, X - 1)], fx_send.at[m])

        @pl.when(s > 0)
        def _():
            await_bytes(ghid.at[m], bg_send.at[m])
            await_bytes(part_in.at[m, pl.ds(0, X - 1)], bx_send.at[m])
            await_bytes(colsum.at[m], bz_send.at[m])

        @pl.when(s == S - 1)
        def _():
            await_bytes(logit_z.at[m, pl.ds(0, Z - 1)], lz_send.at[m])
            await_bytes(logit_x.at[m, pl.ds(0, X - 1)], lx_send.at[m])

        return carry

    lax.fori_loop(0, n, drain, 0)


def on_device(features, labels, weights, vectors, head_weight):
    S, Z, X = lax.axis_size("section"), lax.axis_size("mp_0"), lax.axis_size("mp_1")
    n, R, _ = features.shape
    blocks = Z * X
    bf, f32 = jnp.bfloat16, jnp.float32
    label_rows = jnp.pad(labels[:, None, :], ((0, 0), (0, 0), (0, LANES - R)))
    vmem = pl.BlockSpec(memory_space=pltpu.VMEM)
    dma = pltpu.SemaphoreType.DMA
    wg, nu, coef = pl.pallas_call(
        functools.partial(step_kernel, (S, Z, X, n, R)),
        out_shape=(
            jax.ShapeDtypeStruct((blocks, LANES, LANES), bf),
            jax.ShapeDtypeStruct((1, LANES), f32),
            jax.ShapeDtypeStruct((1, LANES), f32),
        ),
        in_specs=[vmem] * 5,
        out_specs=(vmem, vmem, vmem),
        scratch_shapes=[
            pltpu.VMEM((n, X, Z, R, LANES), bf),
            pltpu.VMEM((n, R, LANES), bf),
            pltpu.VMEM((n, R, LANES), f32),
            pltpu.VMEM((n, R, LANES), bf),
            pltpu.VMEM((n, R, LANES), bf),
            pltpu.VMEM((n, X, Z, R, LANES), bf),
            pltpu.VMEM((n, X, Z, R, LANES), bf),
            pltpu.VMEM((n, Z, R, LANES), bf),
            pltpu.VMEM((n, Z, R, LANES), bf),
            pltpu.VMEM((n, R, LANES), bf),
            pltpu.VMEM((X, Z, 1, LANES), f32),
            pltpu.VMEM((X, Z, 1, LANES), f32),
            pltpu.VMEM((Z, 1, LANES), f32),
            pltpu.VMEM((Z, 1, LANES), f32),
            pltpu.VMEM((X, Z, 1, LANES), f32),
            pltpu.VMEM((Z, 1, LANES), f32),
            pltpu.VMEM((X, 1, LANES), f32),
            pltpu.VMEM((n, Z, 1, LANES), f32),
            pltpu.VMEM((n, X, 1, LANES), f32),
            pltpu.VMEM((Z, 1, LANES), f32),
            pltpu.VMEM((X, 1, LANES), f32),
            pltpu.VMEM((1, LANES), f32),
            dma((8,)),
            dma((8,)),
            dma((n,)),
            dma((n,)),
            dma((n,)),
            dma((n, X)),
            dma((n,)),
            dma((n,)),
            dma((n,)),
            dma((n,)),
            dma((n,)),
            dma((n,)),
            dma((n,)),
            dma((n,)),
            dma((n,)),
            dma((n,)),
        ],
        compiler_params=pltpu.CompilerParams(collective_id=0, has_side_effects=True),
    )(
        features,
        label_rows,
        weights.reshape(blocks, LANES, LANES),
        vectors,
        head_weight[None],
    )
    return wg.reshape(1, blocks * LANES, LANES), nu, coef[0, :1]


def solution(mesh):
    columns = [4 if mesh.shape["mp"] == 64 else 2]
    x_size = columns[0]
    sections = mesh.shape["section"]
    torus = Mesh(
        mesh.devices.reshape(sections, mesh.shape["mp"] // x_size, x_size),
        ("section", "mp_0", "mp_1"),
    )
    placed = (P(None, None, MP), P(), P("section", None, MP), P("section", MP), P(MP))
    return jax.shard_map(
        on_device,
        mesh=torus,
        in_specs=placed,
        out_specs=(P("section", None, MP), P("section", MP), P("section")),
        check_vma=False,
    )
```

time: 1190 us -> 331 us (0.28)
  the two profiles are of different devices: /device:TPU:8 before, /device:TPU:2 now
where the time goes in v1:
time: 331 us; the launch traced here: 330 us
  Pallas kernels  324 us (98%)
  local copies, waits for them, and re-layouts  4.83 us (1%)
    pallas_call x1, Pallas kernels, on_device(): pl.pallas_call(functools.partial(step_kernel, (S, Z, X, n, R)), out_shape...  324 us

profile of v1, /device:TPU:2, one launch (start us, length us, event | category | flops | bytes accessed | tf_op | source)
XLA Modules:
  0.0 330.4 jit_solution(17233643451829427874)
XLA Ops:
  0.6 1.3 pad.4.labels
  1.9 323.7 %shard_map.76 = (bf16[64,128,128]{2,1,0:T(8,128)(2,1)}, f32[1,128]{1,0:T(1,128)}, f32[1,128]{1,0:T(1,128)}) custom-call(bf16[4,32,128]{2,1,0:T(8,128)(2,1)} %feat.1, s32[4,1,128]{2,1,0:T(1,128)} %pad.4.labels, bf16[64,128,128]{2,1,0:T(8,128)(2,1)} %bitcast.8, f32[1,128]{1,0:T(1,128)} %u.1, f32[1,128]{1,0:T(1,128)} %bitcast.11), custom_call_target="tpu_custom_call" | custom-call | tf_op jit(solution)/shard_map/pallas_call | solution.py:394
  325.6 0.0 copy-start.1
  325.6 0.0 copy-start
  325.6 3.0 copy.12
  328.7 0.0 copy-done.1
  328.7 0.5 copy.13
  329.2 0.0 copy-done
Async XLA Ops:
  325.6 3.1 copy-start.1
  325.6 3.6 %copy-start = (f32[1,128]{1,0:T(1,128)S(1)}, f32[1,128]{1,0:T(1,128)}, u32[]{:S(2)}) copy-start(f32[1,128]{1,0:T(1,128)} %get-tuple-element.8) | copy-start | bytes 1540

commit v2 on v1

--- a/solution.py
+++ b/solution.py
@@ -19,8 +19,8 @@
     return gate_val * (1.0 + pre_act * (1.0 - gate_val))
 
 
-def far_first(count):
-    return sorted(range(count), key=lambda d: -min(d, count - d))
+def near_first(count):
+    return sorted(range(count), key=lambda d: min(d, count - d))
 
 
 def remote(src, dst, send, recv, device):
@@ -42,12 +42,14 @@
     dims,
     feat,
     labels,
-    w,
+    w_hbm,
     u,
     head,
     wg_out,
     nu_out,
     coef_out,
+    w,
+    w_sem,
     hid,
     hout,
     pre,
@@ -60,7 +62,6 @@
     gh_in,
     left_x,
     left_xin,
-    left_z,
     left_zin,
     left_all,
     norm_z,
@@ -88,12 +89,17 @@
     lx_recv,
 ):
     S, Z, X, n, R = dims
+    near = near_first(Z)
+    z_far = near[::-1]
+    slot_of = {d: k for k, d in enumerate(near)}
+    groups = [(0, Z // 2), (Z // 2, Z // 4), (Z // 2 + Z // 4, Z // 4)]
+    group_of = [0] * (Z // 2) + [1] * (Z // 4) + [2] * (Z // 4)
     s = lax.axis_index("section")
     z = lax.axis_index("mp_0")
     x = lax.axis_index("mp_1")
     nxt = lax.rem(s + 1, S)
     prv = lax.rem(s + S - 1, S)
-    z_far = far_first(Z)
+    x_far = near_first(X)[:0:-1]
 
     def zat(d):
         return lax.rem(z + d, Z)
@@ -116,6 +122,9 @@
     for d in range(1, X):
         greet((s, z, xat(d)))
 
+    load_w = pltpu.make_async_copy(w_hbm, w, w_sem)
+    load_w.start()
+    z_slot = [zat(d) for d in near]
     u_rows = jnp.broadcast_to(u[...], (16, LANES)).astype(jnp.bfloat16)
 
     def left_block(zi, carry):
@@ -127,6 +136,7 @@
             left_x[xi, zi] = block[0:1]
         return carry
 
+    load_w.wait()
     lax.fori_loop(0, Z, left_block, 0)
     pl.semaphore_wait(barrier, 3 * Z - 1 + X - 1)
 
@@ -134,8 +144,10 @@
     def _():
         def send_features(m, carry):
             for d in z_far:
+                k = slot_of[(Z - d) % Z]
                 remote(
-                    feat.at[m], hid.at[m, x, z], fz_send.at[m], fz_recv.at[m], (nxt, zat(d), x)
+                    feat.at[m], hid.at[m, x, k], fz_send.at[m], fz_recv.at[m, group_of[k]],
+                    (nxt, zat(d), x),
                 ).start()
             return carry
 
@@ -155,29 +167,21 @@
     column = left_x[x]
     for d in range(1, X):
         column = column + left_xin[xat(d)]
-    left_z[...] = column
-    spread_z(lambda d: left_z.at[zat(d)], left_zin.at[z], 1)
+    left_zin[z] = column
+    spread_z(lambda d: left_zin.at[z], left_zin.at[z], 1)
+
+    def forward_columns(m):
+        for g, (first, size) in enumerate(groups):
+            slots = pl.ds(first, size)
+            await_bytes(hid.at[m, x, slots], fz_recv.at[m, g])
+            for d in x_far:
+                remote(
+                    hid.at[m, x, slots], hid.at[m, x, slots], fx_send.at[m], fx_recv.at[m, g],
+                    (s, z, xat(d)),
+                ).start()
+
     await_bytes(left_zin.at[pl.ds(0, Z - 1)], small_recv.at[1])
-    left_zin[z] = left_z[z]
-    left_all[x, z] = jnp.sum(left_zin[...], axis=0)
-    spread_z(lambda d: left_all.at[x, z], left_all.at[x, z], 2)
-
-    def forward_columns(m):
-        await_bytes(hid.at[m, x], fz_recv.at[m])
-        for d in range(1, X):
-            remote(
-                hid.at[m, x], hid.at[m, x], fx_send.at[m], fx_recv.at[m, x], (s, z, xat(d))
-            ).start()
-
-    @pl.when(s == 0)
-    def _():
-        def pass_on(m, carry):
-            forward_columns(m)
-            return carry
-
-        lax.fori_loop(0, n, pass_on, 0)
-
-    await_bytes(left_all.at[0, pl.ds(0, Z - 1)], small_recv.at[2])
+    left_all[x] = jnp.sum(left_zin[...], axis=0)
     spread_x(lambda d: left_all.at[x], left_all.at[x], 3)
     await_bytes(left_all.at[pl.ds(0, X - 1)], small_recv.at[3])
 
@@ -203,16 +207,22 @@
 
     right = lax.fori_loop(0, Z // 2, right_block, jnp.zeros((16, LANES), jnp.float32))[0:1]
 
-    def all_sum(value, zbuf, xbuf, kz, kx):
-        zbuf[z] = value
-        spread_z(lambda d: zbuf.at[z], zbuf.at[z], kz)
-        await_bytes(zbuf.at[pl.ds(0, Z - 1)], small_recv.at[kz])
-        xbuf[x] = jnp.sum(zbuf[...], axis=0)
-        spread_x(lambda d: xbuf.at[x], xbuf.at[x], kx)
-        await_bytes(xbuf.at[pl.ds(0, X - 1)], small_recv.at[kx])
-        return jnp.sum(jnp.sum(xbuf[...], axis=0), axis=-1, keepdims=True)
-
-    norm_total = all_sum(right * right, norm_z, norm_x, 4, 5)
+    norm_z[z] = right * right
+    spread_z(lambda d: norm_z.at[z], norm_z.at[z], 4)
+
+    @pl.when(s == 0)
+    def _():
+        def pass_on(m, carry):
+            forward_columns(m)
+            return carry
+
+        lax.fori_loop(0, n, pass_on, 0)
+
+    await_bytes(norm_z.at[pl.ds(0, Z - 1)], small_recv.at[4])
+    norm_x[x] = jnp.sum(norm_z[...], axis=0)
+    spread_x(lambda d: norm_x.at[x], norm_x.at[x], 5)
+    await_bytes(norm_x.at[pl.ds(0, X - 1)], small_recv.at[5])
+    norm_total = jnp.sum(jnp.sum(norm_x[...], axis=0), axis=-1, keepdims=True)
     inv = 1.0 / jnp.sqrt(norm_total + tiny_eps)
     inv_sig[...] = jnp.broadcast_to(inv, (1, LANES))
     nu_out[...] = right * inv
@@ -222,19 +232,24 @@
         def _():
             forward_columns(m)
 
-        acc = jnp.zeros((R, LANES), jnp.float32)
-        for d in range(X):
+        def partial_dots(acc, d, first, size):
             xi = xat(d)
-            if d:
-                await_bytes(hid.at[m, xi], fx_recv.at[m, xi])
-            for zi in range(0, Z, 2):
-                acc = acc + jnp.dot(
-                    pair([hid[m, xi, zi], hid[m, xi, zi + 1]]), w_pair(xi, zi),
-                    preferred_element_type=jnp.float32,
+            for k in range(first, first + size, 2):
+                rows = jnp.concatenate([hid[m, xi, k], hid[m, xi, k + 1]], axis=1)
+                cols = jnp.concatenate(
+                    [w[z_slot[k] * X + xi], w[z_slot[k + 1] * X + xi]], axis=0
                 )
+                acc = acc + jnp.dot(rows, cols, preferred_element_type=jnp.float32)
+            return acc
+
+        acc = partial_dots(jnp.zeros((R, LANES), jnp.float32), 0, 0, Z)
+        for g, (first, size) in enumerate(groups):
+            await_bytes(hid.at[m, pl.ds(0, X - 1), pl.ds(first, size)], fx_recv.at[m, g])
+            for d in range(1, X):
+                acc = partial_dots(acc, d, first, size)
         pre_act = acc * inv_sig[...]
         pre[m] = pre_act
-        out = (hid[m, x, z].astype(jnp.float32) + pre_act * jax.nn.sigmoid(pre_act)).astype(
+        out = (hid[m, x, 0].astype(jnp.float32) + pre_act * jax.nn.sigmoid(pre_act)).astype(
             jnp.bfloat16
         )
         hout[m] = out
@@ -242,8 +257,10 @@
         @pl.when(s < S - 1)
         def _():
             for d in z_far:
+                k = slot_of[(Z - d) % Z]
                 remote(
-                    hout.at[m], hid.at[m, x, z], fz_send.at[m], fz_recv.at[m], (nxt, zat(d), x)
+                    hout.at[m], hid.at[m, x, k], fz_send.at[m], fz_recv.at[m, group_of[k]],
+                    (nxt, zat(d), x),
                 ).start()
 
         @pl.when(s == S - 1)
@@ -262,8 +279,6 @@
 
         return carry
 
-    lax.fori_loop(0, n, forward_micro, 0)
-
     def backward_micro(m, carry):
         @pl.when(s == S - 1)
         def _():
@@ -276,12 +291,12 @@
                 ).start()
             await_bytes(logit_x.at[m, pl.ds(0, X - 1)], lx_recv.at[m])
             logit_row = jnp.sum(logit_x[m], axis=0)
-            lane = lax.broadcasted_iota(jnp.int32, (R, LANES), 1)
-            row = lax.broadcasted_iota(jnp.int32, (R, LANES), 0)
-            sign_row = (2 * labels[m] - 1).astype(jnp.float32)
-            top_row = -loss_scale * sign_row * jax.nn.sigmoid(-sign_row * logit_row)
+            lane = lax.broadcasted_iota(jnp.int32, (R, R), 1)
+            row = lax.broadcasted_iota(jnp.int32, (R, R), 0)
+            sign_row = (2 * labels[pl.ds(m, 1), :] - 1).astype(jnp.float32)
+            top_row = -loss_scale * sign_row * jax.nn.sigmoid(-sign_row * logit_row[:, :R])
             top = jnp.sum(
-                jnp.where(lane == row, jnp.broadcast_to(top_row, (R, LANES)), 0.0),
+                jnp.where(lane == row, jnp.broadcast_to(top_row, (R, R)), 0.0),
                 axis=1, keepdims=True,
             )
             ghid[m] = (top * head[...]).astype(jnp.bfloat16)
@@ -301,34 +316,54 @@
             remote(
                 ghid.at[m], gh_in.at[m], bg_send.at[m], bg_recv.at[m], (prv, z, x)
             ).start()
-            for d in [*range(1, X), 0]:
-                xi = xat(d)
-                for zi in range(Z):
-                    part[m, xi, zi] = lax.dot_general(
-                        grad, w[zi * X + xi], (((1,), (1,)), ((), ())),
-                        preferred_element_type=jnp.float32,
-                    ).astype(jnp.bfloat16)
-                if d:
+            for g, (first, size) in reversed(list(enumerate(groups))):
+                slots = pl.ds(first, size)
+                for d in [*x_far, 0]:
+                    xi = xat(d)
+                    for k in range(first, first + size):
+                        part[m, xi, k] = lax.dot_general(
+                            grad, w[z_slot[k] * X + xi], (((1,), (1,)), ((), ())),
+                            preferred_element_type=jnp.float32,
+                        ).astype(jnp.bfloat16)
+                    if d:
+                        remote(
+                            part.at[m, xi, slots], part_in.at[m, x, slots], bx_send.at[m],
+                            bx_recv.at[m, g], (s, z, xi),
+                        ).start()
+            for g, (first, size) in reversed(list(enumerate(groups))):
+                await_bytes(
+                    part_in.at[m, pl.ds(0, X - 1), pl.ds(first, size)], bx_recv.at[m, g]
+                )
+                order = range(first + size - 1, first - 1, -1)
+                for k in order:
+                    column_sum = part[m, x, k].astype(jnp.float32)
+                    for e in range(1, X):
+                        column_sum = column_sum + part_in[m, xat(e), k].astype(jnp.float32)
+                    colsum[m, k] = (column_sum * inv_sig[...]).astype(jnp.bfloat16)
+                for k in order:
                     remote(
-                        part.at[m, xi], part_in.at[m, x], bx_send.at[m], bx_recv.at[m],
-                        (s, z, xi),
+                        colsum.at[m, k], col_in.at[m, z], bz_send.at[m], bz_recv.at[m],
+                        (prv, z_slot[k], x),
                     ).start()
-            await_bytes(part_in.at[m, pl.ds(0, X - 1)], bx_recv.at[m])
-            for d in z_far:
-                zi = zat(d)
-                column_sum = part[m, x, zi].astype(jnp.float32)
-                for e in range(1, X):
-                    column_sum = column_sum + part_in[m, xat(e), zi].astype(jnp.float32)
-                colsum[m, zi] = (column_sum * inv_sig[...]).astype(jnp.bfloat16)
-            for d in z_far:
-                zi = zat(d)
-                remote(
-                    colsum.at[m, zi], col_in.at[m, z], bz_send.at[m], bz_recv.at[m], (prv, zi, x)
-                ).start()
 
         return carry
 
-    lax.fori_loop(0, n, backward_micro, 0)
+    @pl.when(s < S - 1)
+    def _():
+        lax.fori_loop(0, n, forward_micro, 0)
+        lax.fori_loop(0, n, backward_micro, 0)
+
+    @pl.when(s == S - 1)
+    def _():
+        forward_micro(0, 0)
+
+        def turn(m, carry):
+            forward_micro(m, carry)
+            backward_micro(m - 1, carry)
+            return carry
+
+        lax.fori_loop(1, n, turn, 0)
+        backward_micro(n - 1, 0)
 
     inner = jnp.sum(gpre[...].astype(jnp.float32) * pre[...], axis=0)
     coef_z[z] = jnp.sum(inner, axis=0, keepdims=True)
@@ -336,16 +371,16 @@
 
     grads = gpre[...].reshape(n * R, LANES)
 
-    def weight_block(zi, carry):
+    def weight_block(k, zi):
         for xi in range(X):
-            rows = hid[:, xi, zi].reshape(n * R, LANES)
+            rows = hid[:, xi, k].reshape(n * R, LANES)
             block = lax.dot_general(
                 rows, grads, (((0,), (0,)), ((), ())), preferred_element_type=jnp.float32
             )
             wg_out[zi * X + xi] = (block * inv_sig[...]).astype(jnp.bfloat16)
-        return carry
-
-    lax.fori_loop(0, Z, weight_block, 0)
+
+    for k in range(Z):
+        weight_block(k, z_slot[k])
 
     await_bytes(coef_z.at[pl.ds(0, Z - 1)], small_recv.at[6])
     coef_x[x] = jnp.sum(coef_z[...], axis=0)
@@ -356,7 +391,6 @@
 
     await_bytes(left_xin.at[pl.ds(0, X - 1)], small_send.at[0])
     await_bytes(left_zin.at[pl.ds(0, Z - 1)], small_send.at[1])
-    await_bytes(left_zin.at[pl.ds(0, Z - 1)], small_send.at[2])
     await_bytes(left_xin.at[pl.ds(0, X - 1)], small_send.at[3])
     for k, buf in ((4, norm_z), (6, coef_z)):
         await_bytes(buf.at[pl.ds(0, Z - 1)], small_send.at[k])
@@ -388,7 +422,6 @@
     n, R, _ = features.shape
     blocks = Z * X
     bf, f32 = jnp.bfloat16, jnp.float32
-    label_rows = jnp.pad(labels[:, None, :], ((0, 0), (0, 0), (0, LANES - R)))
     vmem = pl.BlockSpec(memory_space=pltpu.VMEM)
     dma = pltpu.SemaphoreType.DMA
     wg, nu, coef = pl.pallas_call(
@@ -398,9 +431,11 @@
             jax.ShapeDtypeStruct((1, LANES), f32),
             jax.ShapeDtypeStruct((1, LANES), f32),
         ),
-        in_specs=[vmem] * 5,
+        in_specs=[vmem, vmem, pl.BlockSpec(memory_space=pl.ANY), vmem, vmem],
         out_specs=(vmem, vmem, vmem),
         scratch_shapes=[
+            pltpu.VMEM((blocks, LANES, LANES), bf),
+            dma,
             pltpu.VMEM((n, X, Z, R, LANES), bf),
             pltpu.VMEM((n, R, LANES), bf),
             pltpu.VMEM((n, R, LANES), f32),
@@ -413,8 +448,7 @@
             pltpu.VMEM((n, R, LANES), bf),
             pltpu.VMEM((X, Z, 1, LANES), f32),
             pltpu.VMEM((X, Z, 1, LANES), f32),
-            pltpu.VMEM((Z, 1, LANES), f32),
-            pltpu.VMEM((Z, 1, LANES), f32),
+            pltpu.VMEM((Z, Z, 1, LANES), f32),
             pltpu.VMEM((X, Z, 1, LANES), f32),
             pltpu.VMEM((Z, 1, LANES), f32),
             pltpu.VMEM((X, 1, LANES), f32),
@@ -426,11 +460,11 @@
             dma((8,)),
             dma((8,)),
             dma((n,)),
-            dma((n,)),
-            dma((n,)),
-            dma((n, X)),
-            dma((n,)),
-            dma((n,)),
+            dma((n, 3)),
+            dma((n,)),
+            dma((n, 3)),
+            dma((n,)),
+            dma((n, 3)),
             dma((n,)),
             dma((n,)),
             dma((n,)),
@@ -443,7 +477,7 @@
         compiler_params=pltpu.CompilerParams(collective_id=0, has_side_effects=True),
     )(
         features,
-        label_rows,
+        labels,
         weights.reshape(blocks, LANES, LANES),
         vectors,
         head_weight[None],

time: 331 us -> 293 us (0.89)
  Pallas kernels: 324 us -> 288 us
    pallas_call x1, Pallas kernels: 324 us -> 288 us  [on_device(): pl.pallas_call(functools.partial(step_kernel, (S, Z, X, n, R)), out_shape...]
where the time goes in v2:
time: 293 us
  Pallas kernels  288 us (98%)
  local copies, waits for them, and re-layouts  3.56 us (1%)
    pallas_call x1, Pallas kernels, on_device(): pl.pallas_call(functools.partial(step_kernel, (S, Z, X, n, R)), out_shape...  288 us

profile of v2, /device:TPU:2, one launch (start us, length us, event | category | flops | bytes accessed | tf_op | source)
XLA Modules:
  0.0 293.2 jit_solution(4013533537651279059)
XLA Ops:
  0.6 287.8 %shard_map.76 = (bf16[64,128,128]{2,1,0:T(8,128)(2,1)}, f32[1,128]{1,0:T(1,128)}, f32[1,128]{1,0:T(1,128)}) custom-call(bf16[4,32,128]{2,1,0:T(8,128)(2,1)} %feat.1, s32[4,32]{1,0:T(4,128)} %labels.1, bf16[64,128,128]{2,1,0:T(8,128)(2,1)} %bitcast.5, f32[1,128]{1,0:T(1,128)} %u.1, f32[1,128]{1,0:T(1,128)} %bitcast.7), custom_call_target="tpu_custom_call" | custom-call | tf_op jit(solution)/shard_map/pallas_call | solution.py:427
  288.4 0.0 copy-start.1
  288.4 0.0 copy-start
  288.4 3.0 %copy.11 = bf16[1,8192,128]{2,1,0:T(8,128)(2,1)} copy(bf16[1,8192,128]{2,1,0:T(8,128)(2,1)} %bitcast.6) | data formatting | bytes 4194304
  291.5 0.0 copy-done.1
  291.5 0.5 copy.12
  292.0 0.0 copy-done
Async XLA Ops:
  288.4 3.1 %copy-start.1 = (f32[1,128]{1,0:T(1,128)S(1)}, f32[1,128]{1,0:T(1,128)}, u32[]{:S(2)}) copy-start(f32[1,128]{1,0:T(1,128)} %get-tuple-element.13) | copy-start | bytes 1540
  288.4 3.6 %copy-start = (f32[1,128]{1,0:T(1,128)S(1)}, f32[1,128]{1,0:T(1,128)}, u32[]{:S(2)}) copy-start(f32[1,128]{1,0:T(1,128)} %get-tuple-element.8) | copy-start | bytes 1540

commit v3 on v2

--- a/solution.py
+++ b/solution.py
@@ -64,12 +64,9 @@
     left_xin,
     left_zin,
     left_all,
-    norm_z,
-    norm_x,
-    logit_z,
-    logit_x,
-    coef_z,
-    coef_x,
+    norms,
+    logits,
+    coefs,
     inv_sig,
     small_send,
     small_recv,
@@ -85,8 +82,6 @@
     bg_recv,
     lz_send,
     lz_recv,
-    lx_send,
-    lx_recv,
 ):
     S, Z, X, n, R = dims
     near = near_first(Z)
@@ -101,6 +96,9 @@
     prv = lax.rem(s + S - 1, S)
     x_far = near_first(X)[:0:-1]
 
+    peers = [(d, e) for d in z_far for e in range(X) if d or e]
+    me = z * X + x
+
     def zat(d):
         return lax.rem(z + d, Z)
 
@@ -117,10 +115,8 @@
     for d in z_far:
         greet((nxt, zat(d), x))
         greet((prv, zat(d), x))
-        if d:
-            greet((s, zat(d), x))
-    for d in range(1, X):
-        greet((s, z, xat(d)))
+    for d, e in peers:
+        greet((s, zat(d), xat(e)))
 
     load_w = pltpu.make_async_copy(w_hbm, w, w_sem)
     load_w.start()
@@ -138,7 +134,7 @@
 
     load_w.wait()
     lax.fori_loop(0, Z, left_block, 0)
-    pl.semaphore_wait(barrier, 3 * Z - 1 + X - 1)
+    pl.semaphore_wait(barrier, 2 * Z + len(peers))
 
     @pl.when(s == S - 1)
     def _():
@@ -158,6 +154,10 @@
             if d:
                 remote(src(d), dst, small_send.at[k], small_recv.at[k], (s, zat(d), x)).start()
 
+    def share(row, send, recv):
+        for d, e in peers:
+            remote(row, row, send, recv, (s, zat(d), xat(e))).start()
+
     def spread_x(src, dst, k):
         for d in range(1, X):
             remote(src(d), dst, small_send.at[k], small_recv.at[k], (s, z, xat(d))).start()
@@ -207,8 +207,8 @@
 
     right = lax.fori_loop(0, Z // 2, right_block, jnp.zeros((16, LANES), jnp.float32))[0:1]
 
-    norm_z[z] = right * right
-    spread_z(lambda d: norm_z.at[z], norm_z.at[z], 4)
+    norms[me] = right * right
+    share(norms.at[me], small_send.at[4], small_recv.at[4])
 
     @pl.when(s == 0)
     def _():
@@ -218,20 +218,18 @@
 
         lax.fori_loop(0, n, pass_on, 0)
 
-    await_bytes(norm_z.at[pl.ds(0, Z - 1)], small_recv.at[4])
-    norm_x[x] = jnp.sum(norm_z[...], axis=0)
-    spread_x(lambda d: norm_x.at[x], norm_x.at[x], 5)
-    await_bytes(norm_x.at[pl.ds(0, X - 1)], small_recv.at[5])
-    norm_total = jnp.sum(jnp.sum(norm_x[...], axis=0), axis=-1, keepdims=True)
+    await_bytes(norms.at[pl.ds(0, Z * X - 1)], small_recv.at[4])
+    norm_total = jnp.sum(jnp.sum(norms[...], axis=0), axis=-1, keepdims=True)
     inv = 1.0 / jnp.sqrt(norm_total + tiny_eps)
     inv_sig[...] = jnp.broadcast_to(inv, (1, LANES))
     nu_out[...] = right * inv
 
-    def forward_micro(m, carry):
+    def forward_start(m):
         @pl.when(s > 0)
         def _():
             forward_columns(m)
 
+    def forward_end(m):
         def partial_dots(acc, d, first, size):
             xi = xat(d)
             for k in range(first, first + size, 2):
@@ -269,28 +267,14 @@
             lane = lax.broadcasted_iota(jnp.int32, (R, LANES), 1)
             row = lax.broadcasted_iota(jnp.int32, (R, LANES), 0)
             spread = jnp.where(lane == row, jnp.broadcast_to(terms, (R, LANES)), 0.0)
-            logit_z[m, z] = jnp.sum(spread, axis=0, keepdims=True)
-            for d in z_far:
-                if d:
-                    remote(
-                        logit_z.at[m, z], logit_z.at[m, z], lz_send.at[m], lz_recv.at[m],
-                        (s, zat(d), x),
-                    ).start()
-
-        return carry
-
-    def backward_micro(m, carry):
+            logits[m, me] = jnp.sum(spread, axis=0, keepdims=True)
+            share(logits.at[m, me], lz_send.at[m], lz_recv.at[m])
+
+    def backward_start(m):
         @pl.when(s == S - 1)
         def _():
-            await_bytes(logit_z.at[m, pl.ds(0, Z - 1)], lz_recv.at[m])
-            logit_x[m, x] = jnp.sum(logit_z[m], axis=0)
-            for d in range(1, X):
-                remote(
-                    logit_x.at[m, x], logit_x.at[m, x], lx_send.at[m], lx_recv.at[m],
-                    (s, z, xat(d)),
-                ).start()
-            await_bytes(logit_x.at[m, pl.ds(0, X - 1)], lx_recv.at[m])
-            logit_row = jnp.sum(logit_x[m], axis=0)
+            await_bytes(logits.at[m, pl.ds(0, Z * X - 1)], lz_recv.at[m])
+            logit_row = jnp.sum(logits[m], axis=0)
             lane = lax.broadcasted_iota(jnp.int32, (R, R), 1)
             row = lax.broadcasted_iota(jnp.int32, (R, R), 0)
             sign_row = (2 * labels[pl.ds(m, 1), :] - 1).astype(jnp.float32)
@@ -330,6 +314,10 @@
                             part.at[m, xi, slots], part_in.at[m, x, slots], bx_send.at[m],
                             bx_recv.at[m, g], (s, z, xi),
                         ).start()
+
+    def backward_end(m):
+        @pl.when(s > 0)
+        def _():
             for g, (first, size) in reversed(list(enumerate(groups))):
                 await_bytes(
                     part_in.at[m, pl.ds(0, X - 1), pl.ds(first, size)], bx_recv.at[m, g]
@@ -346,28 +334,35 @@
                         (prv, z_slot[k], x),
                     ).start()
 
+    def forward_turn(m, carry):
+        forward_start(m + 1)
+        forward_end(m)
         return carry
+
+    def backward_turn(m, carry):
+        backward_start(m + 1)
+        backward_end(m)
+        return carry
+
+    forward_start(0)
+    lax.fori_loop(0, n - 1, forward_turn, 0)
+
+    @pl.when(s == S - 1)
+    def _():
+        backward_start(0)
+
+    forward_end(n - 1)
 
     @pl.when(s < S - 1)
     def _():
-        lax.fori_loop(0, n, forward_micro, 0)
-        lax.fori_loop(0, n, backward_micro, 0)
-
-    @pl.when(s == S - 1)
-    def _():
-        forward_micro(0, 0)
-
-        def turn(m, carry):
-            forward_micro(m, carry)
-            backward_micro(m - 1, carry)
-            return carry
-
-        lax.fori_loop(1, n, turn, 0)
-        backward_micro(n - 1, 0)
+        backward_start(0)
+
+    lax.fori_loop(0, n - 1, backward_turn, 0)
+    backward_end(n - 1)
 
     inner = jnp.sum(gpre[...].astype(jnp.float32) * pre[...], axis=0)
-    coef_z[z] = jnp.sum(inner, axis=0, keepdims=True)
-    spread_z(lambda d: coef_z.at[z], coef_z.at[z], 6)
+    coefs[me] = jnp.sum(inner, axis=0, keepdims=True)
+    share(coefs.at[me], small_send.at[6], small_recv.at[6])
 
     grads = gpre[...].reshape(n * R, LANES)
 
@@ -382,20 +377,15 @@
     for k in range(Z):
         weight_block(k, z_slot[k])
 
-    await_bytes(coef_z.at[pl.ds(0, Z - 1)], small_recv.at[6])
-    coef_x[x] = jnp.sum(coef_z[...], axis=0)
-    spread_x(lambda d: coef_x.at[x], coef_x.at[x], 7)
-    await_bytes(coef_x.at[pl.ds(0, X - 1)], small_recv.at[7])
-    inner_total = jnp.sum(jnp.sum(coef_x[...], axis=0), axis=-1, keepdims=True)
+    await_bytes(coefs.at[pl.ds(0, Z * X - 1)], small_recv.at[6])
+    inner_total = jnp.sum(jnp.sum(coefs[...], axis=0), axis=-1, keepdims=True)
     coef_out[...] = inner_total * inv_sig[...]
 
     await_bytes(left_xin.at[pl.ds(0, X - 1)], small_send.at[0])
     await_bytes(left_zin.at[pl.ds(0, Z - 1)], small_send.at[1])
     await_bytes(left_xin.at[pl.ds(0, X - 1)], small_send.at[3])
-    for k, buf in ((4, norm_z), (6, coef_z)):
-        await_bytes(buf.at[pl.ds(0, Z - 1)], small_send.at[k])
-    for k, buf in ((5, norm_x), (7, coef_x)):
-        await_bytes(buf.at[pl.ds(0, X - 1)], small_send.at[k])
+    await_bytes(norms.at[pl.ds(0, Z * X - 1)], small_send.at[4])
+    await_bytes(coefs.at[pl.ds(0, Z * X - 1)], small_send.at[6])
 
     def drain(m, carry):
         await_bytes(hid.at[m, 0], fz_send.at[m])
@@ -409,8 +399,7 @@
 
         @pl.when(s == S - 1)
         def _():
-            await_bytes(logit_z.at[m, pl.ds(0, Z - 1)], lz_send.at[m])
-            await_bytes(logit_x.at[m, pl.ds(0, X - 1)], lx_send.at[m])
+            await_bytes(logits.at[m, pl.ds(0, Z * X - 1)], lz_send.at[m])
 
         return carry
 
@@ -450,12 +439,9 @@
             pltpu.VMEM((X, Z, 1, LANES), f32),
             pltpu.VMEM((Z, Z, 1, LANES), f32),
             pltpu.VMEM((X, Z, 1, LANES), f32),
-            pltpu.VMEM((Z, 1, LANES), f32),
-            pltpu.VMEM((X, 1, LANES), f32),
-            pltpu.VMEM((n, Z, 1, LANES), f32),
-            pltpu.VMEM((n, X, 1, LANES), f32),
-            pltpu.VMEM((Z, 1, LANES), f32),
-            pltpu.VMEM((X, 1, LANES), f32),
+            pltpu.VMEM((blocks, 1, LANES), f32),
+            pltpu.VMEM((n, blocks, 1, LANES), f32),
+            pltpu.VMEM((blocks, 1, LANES), f32),
             pltpu.VMEM((1, LANES), f32),
             dma((8,)),
             dma((8,)),
@@ -465,8 +451,6 @@
             dma((n, 3)),
             dma((n,)),
             dma((n, 3)),
-            dma((n,)),
-            dma((n,)),
             dma((n,)),
             dma((n,)),
             dma((n,)),

time: 293 us -> 263 us (0.90)
  the two profiles are of different devices: /device:TPU:2 before, /device:TPU:32 now
where the time goes in v3:
time: 263 us
  Pallas kernels  258 us (98%)
  local copies, waits for them, and re-layouts  3.56 us (1%)
    pallas_call x1, Pallas kernels, on_device(): pl.pallas_call(functools.partial(step_kernel, (S, Z, X, n, R)), out_shape...  258 us

profile of v3, /device:TPU:32, one launch (start us, length us, event | category | flops | bytes accessed | tf_op | source)
XLA Modules:
  0.0 263.0 jit_solution(10401676844347492272)
XLA Ops:
  0.6 257.7 %shard_map.76 = (bf16[64,128,128]{2,1,0:T(8,128)(2,1)}, f32[1,128]{1,0:T(1,128)}, f32[1,128]{1,0:T(1,128)}) custom-call(bf16[4,32,128]{2,1,0:T(8,128)(2,1)} %feat.1, s32[4,32]{1,0:T(4,128)} %labels.1, bf16[64,128,128]{2,1,0:T(8,128)(2,1)} %bitcast.5, f32[1,128]{1,0:T(1,128)} %u.1, f32[1,128]{1,0:T(1,128)} %bitcast.7), custom_call_target="tpu_custom_call" | custom-call | tf_op jit(solution)/shard_map/pallas_call | solution.py:416
  258.3 0.0 copy-start.1
  258.3 0.0 copy-start
  258.3 3.0 %copy.11 = bf16[1,8192,128]{2,1,0:T(8,128)(2,1)} copy(bf16[1,8192,128]{2,1,0:T(8,128)(2,1)} %bitcast.6) | data formatting | bytes 4194304
  261.4 0.0 copy-done.1
  261.4 0.5 copy.12
  261.9 0.0 copy-done
Async XLA Ops:
  258.3 3.1 %copy-start.1 = (f32[1,128]{1,0:T(1,128)S(1)}, f32[1,128]{1,0:T(1,128)}, u32[]{:S(2)}) copy-start(f32[1,128]{1,0:T(1,128)} %get-tuple-element.13) | copy-start | bytes 1540
  258.3 3.6 %copy-start = (f32[1,128]{1,0:T(1,128)S(1)}, f32[1,128]{1,0:T(1,128)}, u32[]{:S(2)}) copy-start(f32[1,128]{1,0:T(1,128)} %get-tuple-element.8) | copy-start | bytes 1540

commit v4 on v3

--- a/solution.py
+++ b/solution.py
@@ -334,31 +334,31 @@
                         (prv, z_slot[k], x),
                     ).start()
 
-    def forward_turn(m, carry):
-        forward_start(m + 1)
-        forward_end(m)
+    turns_apart = jnp.where(s == S - 1, min(3, n), n)
+
+    def turn(t, carry):
+        back = t - turns_apart
+
+        @pl.when(t + 1 < n)
+        def _():
+            forward_start(t + 1)
+
+        @pl.when((back >= 0) & (back < n))
+        def _():
+            backward_start(back)
+
+        @pl.when(t < n)
+        def _():
+            forward_end(t)
+
+        @pl.when((back >= 1) & (back <= n))
+        def _():
+            backward_end(back - 1)
+
         return carry
 
-    def backward_turn(m, carry):
-        backward_start(m + 1)
-        backward_end(m)
-        return carry
-
     forward_start(0)
-    lax.fori_loop(0, n - 1, forward_turn, 0)
-
-    @pl.when(s == S - 1)
-    def _():
-        backward_start(0)
-
-    forward_end(n - 1)
-
-    @pl.when(s < S - 1)
-    def _():
-        backward_start(0)
-
-    lax.fori_loop(0, n - 1, backward_turn, 0)
-    backward_end(n - 1)
+    lax.fori_loop(0, 2 * n + 1, turn, 0)
 
     inner = jnp.sum(gpre[...].astype(jnp.float32) * pre[...], axis=0)
     coefs[me] = jnp.sum(inner, axis=0, keepdims=True)
@@ -409,6 +409,9 @@
 def on_device(features, labels, weights, vectors, head_weight):
     S, Z, X = lax.axis_size("section"), lax.axis_size("mp_0"), lax.axis_size("mp_1")
     n, R, _ = features.shape
+    features = features.reshape(n * 2, R // 2, LANES)
+    labels = labels.reshape(n * 2, R // 2)
+    n, R = n * 2, R // 2
     blocks = Z * X
     bf, f32 = jnp.bfloat16, jnp.float32
     vmem = pl.BlockSpec(memory_space=pltpu.VMEM)
@@ -416,9 +419,9 @@
     wg, nu, coef = pl.pallas_call(
         functools.partial(step_kernel, (S, Z, X, n, R)),
         out_shape=(
-            jax.ShapeDtypeStruct((blocks, LANES, LANES), bf),
-            jax.ShapeDtypeStruct((1, LANES), f32),
-            jax.ShapeDtypeStruct((1, LANES), f32),
+            pltpu.VMEM((blocks, LANES, LANES), bf),
+            pltpu.VMEM((1, LANES), f32),
+            pltpu.VMEM((1, LANES), f32),
         ),
         in_specs=[vmem, vmem, pl.BlockSpec(memory_space=pl.ANY), vmem, vmem],
         out_specs=(vmem, vmem, vmem),

time: 263 us -> 250 us (0.951)
  the two profiles are of different devices: /device:TPU:32 before, /device:TPU:2 now
where the time goes in v4:
time: 250 us; the launch traced here: 249 us
  Pallas kernels  244 us (98%)
  local copies, waits for them, and re-layouts  3.18 us (1%)
    pallas_call x1, Pallas kernels, on_device(): pl.pallas_call(functools.partial(step_kernel, (S, Z, X, n, R)), out_shape...  244 us

profile of v4, /device:TPU:2, one launch (start us, length us, event | category | flops | bytes accessed | tf_op | source)
XLA Modules:
  0.0 249.4 jit_solution(627504219310084386)
XLA Ops:
  0.6 1.3 reshape.19.labels
  2.0 244.4 %shard_map.76 = (bf16[64,128,128]{2,1,0:T(8,128)(2,1)S(1)}, f32[1,128]{1,0:T(1,128)S(1)}, f32[1,128]{1,0:T(1,128)S(1)}) custom-call(bf16[8,16,128]{2,1,0:T(8,128)(2,1)} %bitcast.9, s32[8,16]{1,0:T(8,128)} %reshape.19.labels, bf16[64,128,128]{2,1,0:T(8,128)(2,1)} %bitcast.8, f32[1,128]{1,0:T(1,128)} %u.1, f32[1,128]{1,0:T(1,128)} %bitcast.10), custom_call_target="tpu_custom_call" | custom-call | tf_op jit(solution)/shard_map/pallas_call | solution.py:419
  246.4 1.3 copy.11
  247.7 0.5 copy.12

commit v5 on v4

--- a/solution.py
+++ b/solution.py
@@ -49,6 +49,7 @@
     nu_out,
     coef_out,
     w,
+    w_turned,
     w_sem,
     hid,
     hout,
@@ -125,10 +126,9 @@
 
     def left_block(zi, carry):
         for xi in range(X):
-            block = lax.dot_general(
-                u_rows, w[zi * X + xi], (((1,), (1,)), ((), ())),
-                preferred_element_type=jnp.float32,
-            )
+            turned = w[zi * X + xi].T
+            w_turned[zi * X + xi] = turned
+            block = jnp.dot(u_rows, turned, preferred_element_type=jnp.float32)
             left_x[xi, zi] = block[0:1]
         return carry
 
@@ -136,18 +136,20 @@
     lax.fori_loop(0, Z, left_block, 0)
     pl.semaphore_wait(barrier, 2 * Z + len(peers))
 
+    def send_features(m, carry):
+        for d in z_far:
+            k = slot_of[(Z - d) % Z]
+            remote(
+                feat.at[m], hid.at[m, x, k], fz_send.at[m], fz_recv.at[m, group_of[k]],
+                (nxt, zat(d), x),
+            ).start()
+        return carry
+
+    early = min(2, n)
+
     @pl.when(s == S - 1)
     def _():
-        def send_features(m, carry):
-            for d in z_far:
-                k = slot_of[(Z - d) % Z]
-                remote(
-                    feat.at[m], hid.at[m, x, k], fz_send.at[m], fz_recv.at[m, group_of[k]],
-                    (nxt, zat(d), x),
-                ).start()
-            return carry
-
-        lax.fori_loop(0, n, send_features, 0)
+        lax.fori_loop(0, early, send_features, 0)
 
     def spread_z(src, dst, k):
         for d in z_far:
@@ -183,6 +185,11 @@
     await_bytes(left_zin.at[pl.ds(0, Z - 1)], small_recv.at[1])
     left_all[x] = jnp.sum(left_zin[...], axis=0)
     spread_x(lambda d: left_all.at[x], left_all.at[x], 3)
+
+    @pl.when(s == S - 1)
+    def _():
+        lax.fori_loop(early, n, send_features, 0)
+
     await_bytes(left_all.at[pl.ds(0, X - 1)], small_recv.at[3])
 
     left = left_all[...]
@@ -216,18 +223,13 @@
             forward_columns(m)
             return carry
 
-        lax.fori_loop(0, n, pass_on, 0)
+        lax.fori_loop(0, early, pass_on, 0)
 
     await_bytes(norms.at[pl.ds(0, Z * X - 1)], small_recv.at[4])
     norm_total = jnp.sum(jnp.sum(norms[...], axis=0), axis=-1, keepdims=True)
     inv = 1.0 / jnp.sqrt(norm_total + tiny_eps)
     inv_sig[...] = jnp.broadcast_to(inv, (1, LANES))
     nu_out[...] = right * inv
-
-    def forward_start(m):
-        @pl.when(s > 0)
-        def _():
-            forward_columns(m)
 
     def forward_end(m):
         def partial_dots(acc, d, first, size):
@@ -275,14 +277,21 @@
         def _():
             await_bytes(logits.at[m, pl.ds(0, Z * X - 1)], lz_recv.at[m])
             logit_row = jnp.sum(logits[m], axis=0)
-            lane = lax.broadcasted_iota(jnp.int32, (R, R), 1)
-            row = lax.broadcasted_iota(jnp.int32, (R, R), 0)
-            sign_row = (2 * labels[pl.ds(m, 1), :] - 1).astype(jnp.float32)
-            top_row = -loss_scale * sign_row * jax.nn.sigmoid(-sign_row * logit_row[:, :R])
-            top = jnp.sum(
-                jnp.where(lane == row, jnp.broadcast_to(top_row, (R, R)), 0.0),
-                axis=1, keepdims=True,
-            )
+
+            def as_column(row_vals, offset):
+                width = row_vals.shape[1]
+                lane = lax.broadcasted_iota(jnp.int32, (R, width), 1)
+                row = lax.broadcasted_iota(jnp.int32, (R, width), 0)
+                spread = jnp.broadcast_to(row_vals, (R, width))
+                return jnp.sum(
+                    jnp.where(lane == row + offset, spread, 0.0), axis=1, keepdims=True
+                )
+
+            cuts = labels.shape[1] // R
+            label_row = labels[pl.ds(m // cuts, 1), :].astype(jnp.float32)
+            sign = 2.0 * as_column(label_row, lax.rem(m, cuts) * R) - 1.0
+            logit = as_column(logit_row, 0)
+            top = -loss_scale * sign * jax.nn.sigmoid(-sign * logit)
             ghid[m] = (top * head[...]).astype(jnp.bfloat16)
 
         @pl.when(s < S - 1)
@@ -305,8 +314,8 @@
                 for d in [*x_far, 0]:
                     xi = xat(d)
                     for k in range(first, first + size):
-                        part[m, xi, k] = lax.dot_general(
-                            grad, w[z_slot[k] * X + xi], (((1,), (1,)), ((), ())),
+                        part[m, xi, k] = jnp.dot(
+                            grad, w_turned[z_slot[k] * X + xi],
                             preferred_element_type=jnp.float32,
                         ).astype(jnp.bfloat16)
                     if d:
@@ -339,9 +348,9 @@
     def turn(t, carry):
         back = t - turns_apart
 
-        @pl.when(t + 1 < n)
-        def _():
-            forward_start(t + 1)
+        @pl.when(t + ahead < n)
+        def _():
+            forward_columns(t + ahead)
 
         @pl.when((back >= 0) & (back < n))
         def _():
@@ -357,7 +366,12 @@
 
         return carry
 
-    forward_start(0)
+    ahead = jnp.where(s == 0, early, 1)
+
+    @pl.when(s > 0)
+    def _():
+        forward_columns(0)
+
     lax.fori_loop(0, 2 * n + 1, turn, 0)
 
     inner = jnp.sum(gpre[...].astype(jnp.float32) * pre[...], axis=0)
@@ -410,7 +424,6 @@
     S, Z, X = lax.axis_size("section"), lax.axis_size("mp_0"), lax.axis_size("mp_1")
     n, R, _ = features.shape
     features = features.reshape(n * 2, R // 2, LANES)
-    labels = labels.reshape(n * 2, R // 2)
     n, R = n * 2, R // 2
     blocks = Z * X
     bf, f32 = jnp.bfloat16, jnp.float32
@@ -426,6 +439,7 @@
         in_specs=[vmem, vmem, pl.BlockSpec(memory_space=pl.ANY), vmem, vmem],
         out_specs=(vmem, vmem, vmem),
         scratch_shapes=[
+            pltpu.VMEM((blocks, LANES, LANES), bf),
             pltpu.VMEM((blocks, LANES, LANES), bf),
             dma,
             pltpu.VMEM((n, X, Z, R, LANES), bf),

time: 250 us -> 242 us (0.968)
  Pallas kernels: 244 us -> 238 us
    pallas_call x1, Pallas kernels: 244 us -> 238 us  [on_device(): pl.pallas_call(functools.partial(step_kernel, (S, Z, X, n, R)), out_shape...]
where the time goes in v5:
time: 242 us
  Pallas kernels  238 us (98%)
    pallas_call x1, Pallas kernels, on_device(): pl.pallas_call(functools.partial(step_kernel, (S, Z, X, n, R)), out_shape...  238 us

profile of v5, /device:TPU:2, one launch (start us, length us, event | category | flops | bytes accessed | tf_op | source)
XLA Modules:
  0.0 241.9 jit_solution(8812170288933035943)
XLA Ops:
  0.6 238.3 %shard_map.76 = (bf16[64,128,128]{2,1,0:T(8,128)(2,1)S(1)}, f32[1,128]{1,0:T(1,128)S(1)}, f32[1,128]{1,0:T(1,128)S(1)}) custom-call(bf16[8,16,128]{2,1,0:T(8,128)(2,1)} %bitcast.9, s32[4,32]{1,0:T(4,128)} %labels.1, bf16[64,128,128]{2,1,0:T(8,128)(2,1)} %bitcast.8, f32[1,128]{1,0:T(1,128)} %u.1, f32[1,128]{1,0:T(1,128)} %bitcast.10), custom_call_target="tpu_custom_call" | custom-call | tf_op jit(solution)/shard_map/pallas_call | solution.py:432
  238.9 1.3 copy.11
  240.3 0.5 copy.12
